TPU v7x, 512 devices: a whole 4x4x16 slice. The times are simulated.
512 devices in a mesh: rep: 32 (over y, x, core), tp: 16 (over z).
Axes of the slice: x: 4, y: 4, z: 16, core: 2. Of those that a mesh axis runs over, the one named last changes fastest.
Arguments:
- tokens: bfloat16 [512, 1024], P('rep'), may hold values from -6 to 6
- lengths: int32 [512], P('rep'), may hold values from 1 to 256, as said below
- prompt_group: int32 [512], P('rep'), may hold values from 0 to 7
- span_close: int32 [512], P('rep'), may hold values 0 or 1
- out_slot: int32 [32, 2], P('rep'), may hold values from 0 to 15, as said below
- move_dest: int32 [32, 2], P('rep'), may hold values from 0 to 31, as said below
- page_table: int32 [512, 2, 1], P('rep'), may hold values from 0 to 15, as said below
- cache_pool: bfloat16 [512, 16, 128, 256], P('rep', 'tp'), may hold values from -6 to 6
- prefix_cache: bfloat16 [8, 16, 64, 256], P(None, 'tp'), may hold values from -6 to 6
- memory: float32 [512, 16, 64, 128], P('rep', 'tp'), may hold values from -2 to 2
- norm_attn: float32 [1024], replicated, may hold values from 0.5 to 1.5
- norm_mlp: float32 [1024], replicated, may hold values from 0.5 to 1.5
- qkv_weight: bfloat16 [1024, 3072], P(None, 'tp'), may hold values from -0.1875 to 0.1875
- out_weight: bfloat16 [1024, 1024], P('tp'), may hold values from -0.1875 to 0.1875
- gate_weight: bfloat16 [1024, 2816], P(None, 'tp'), may hold values from -0.1875 to 0.1875
- up_weight: bfloat16 [1024, 2816], P(None, 'tp'), may hold values from -0.1875 to 0.1875
- down_weight: bfloat16 [2816, 1024], P('tp'), may hold values from -0.109375 to 0.109375
- forget: float32 [8], replicated, may hold values from 0.5 to 0.99
- write_rate: float32 [8], replicated, may hold values from 0.1 to 0.9
Outputs:
- out_rows: bfloat16 [512, 1024], P('rep')
- new_memory: float32 [512, 16, 64, 128], P('rep', 'tp')
- new_cache_pool: bfloat16 [512, 16, 128, 256], P('rep', 'tp')
Inputs may be any that keep to these rules, and one draw needn't show every extreme that they name: `lengths`: the cached tokens of a request; some request of every replica holds 256. `out_slot`: the 2 slots of one replica are distinct. For each m, move_dest[:, m] is a permutation of the replicas. `page_table`: for each replica and half, the entries of its 16 slots are a permutation of 0 to 15.
All inputs are finite; a program needn't handle non-finite values. No bound on the sum of `span_close` on one device may be relied on, other than what follows from the above.
Results may differ from a plain program's by a relative error of at most 0.013.
Values may be sent and summed in bfloat16 or wider, within the bound.
No kernel may reach another device: no remote copies, remote signals or barrier semaphores. Data moves between devices by JAX's collectives and lax.ppermute only.
A program may use at most 64 MiB of HBM per device.

v0:
```python
import jax
import jax.numpy as jnp
from jax import lax
from jax.sharding import PartitionSpec as P

highest = lax.Precision.HIGHEST


def from_partner(block, axis, apart):
    count = lax.axis_size(axis)
    route = []
    for low in range(count):
        high = low | 1 << apart
        if high != low and high < count:
            route += [(low, high), (high, low)]
    return lax.ppermute(block, axis, route)


def rms_scale(values, gain_vec):
    return values * lax.rsqrt(jnp.mean(values * values, axis=-1, keepdims=True) + 1e-05) * gain_vec


def unit_rows(values):
    return values * lax.rsqrt(jnp.sum(values * values, axis=-1, keepdims=True) + 1e-06)


def join_pair(part_one, part_two):
    top_one, denom_one, accum_one = part_one
    top_two, denom_two, accum_two = part_two
    top_score = jnp.maximum(top_one, top_two)
    weight_one = jnp.exp(top_one - top_score)
    weight_two = jnp.exp(top_two - top_score)
    return (
        top_score,
        denom_one * weight_one + denom_two * weight_two,
        accum_one * weight_one[..., None] + accum_two * weight_two[..., None],
    )


def picked_rows(dest_rows, my_rep, move_count):
    row_count = dest_rows.shape[0]
    row_move = jnp.arange(row_count) % move_count
    return (dest_rows == my_rep)[:, None] & (row_move[:, None] == jnp.arange(move_count)[None, :])


def body(
    tokens,
    lengths,
    prompt_group,
    span_close,
    out_slot,
    move_dest,
    page_table,
    cache_pool,
    prefix_cache,
    memory,
    norm_attn,
    norm_mlp,
    qkv_weight,
    out_weight,
    gate_weight,
    up_weight,
    down_weight,
    forget,
    write_rate,
):
    req_count = tokens.shape[0]
    model_dim = tokens.shape[1]
    sect_count = cache_pool.shape[1]
    page_len = cache_pool.shape[2]
    half_dim = memory.shape[2]
    head_dim = memory.shape[3]
    head_count = forget.shape[0]
    group_count = prefix_cache.shape[0]
    move_count = out_slot.shape[1]
    page_count = page_table.shape[2]
    sections = lax.axis_index("tp") * sect_count + jnp.arange(sect_count)
    halves = sections // head_count
    head_ids = sections % head_count
    sect_index = jnp.arange(sect_count)[None, :, None]
    moved_slots = out_slot[0]
    page_ids = page_table[:, halves, :]
    slot_pages = page_ids[moved_slots]
    my_rep = lax.axis_index("rep")
    send_pages = cache_pool[slot_pages, sect_index].reshape(move_count, -1)
    dest_rows = lax.all_gather(move_dest[0], "rep", axis=0, tiled=True)
    page_rows = lax.all_gather(send_pages, "rep", axis=0, tiled=True)
    picked = picked_rows(dest_rows, my_rep, move_count)
    pages_in = jnp.dot(picked.astype(jnp.bfloat16).T, page_rows, preferred_element_type=jnp.float32)
    new_pool = cache_pool.at[slot_pages, sect_index].set(
        pages_in.astype(jnp.bfloat16).reshape(
            move_count, sect_count, page_count, page_len, 2 * head_dim
        )
    )
    residual_in = tokens.astype(jnp.float32)
    normed = rms_scale(residual_in, norm_attn).astype(jnp.bfloat16)
    qkv_part = jnp.dot(normed, qkv_weight, preferred_element_type=jnp.float32).astype(jnp.bfloat16)
    qkv_full = lax.all_gather(qkv_part, "tp", axis=1, tiled=True)
    queries = qkv_full[:, :model_dim].reshape(req_count, head_count, head_dim)[:, head_ids]
    keys_new = qkv_full[:, model_dim : 2 * model_dim].reshape(req_count, head_count, head_dim)[
        :, head_ids
    ]
    values_new = qkv_full[:, 2 * model_dim :].reshape(req_count, head_count, head_dim)[:, head_ids]
    score_scale = head_dim ** (-0.5)
    cached = cache_pool[page_ids, sect_index].reshape(req_count, sect_count, -1, 2 * head_dim)
    group_hot = (prompt_group[:, None] == jnp.arange(group_count)[None, :]).astype(jnp.bfloat16)
    prefix = jnp.einsum(
        "rg,gsnd->rsnd", group_hot, prefix_cache, preferred_element_type=jnp.float32
    ).astype(jnp.bfloat16)
    key_data = jnp.concatenate([prefix, cached], axis=2)
    positions = (
        (2 * jnp.arange(page_count)[None, :, None] + halves[:, None, None]) * page_len
        + jnp.arange(page_len)[None, None, :]
    ).reshape(sect_count, -1)
    live_keys = jnp.concatenate(
        [
            jnp.ones((req_count, sect_count, prefix.shape[2]), bool),
            positions[None, :, :] < lengths[:, None, None],
        ],
        axis=2,
    )
    scores = (
        jnp.einsum(
            "rsd,rsnd->rsn", queries, key_data[..., :head_dim], preferred_element_type=jnp.float32
        )
        * score_scale
    )
    scores = jnp.where(live_keys, scores, -jnp.inf)
    query_full = queries.astype(jnp.float32)
    key_full = keys_new.astype(jnp.float32)
    value_full = values_new.astype(jnp.float32)
    own_score = jnp.sum(query_full * key_full, axis=-1) * score_scale
    own_score = jnp.where(halves[None, :] == 0, own_score, -jnp.inf)
    top_score = jnp.maximum(jnp.max(scores, axis=-1), own_score)
    weights = jnp.exp(scores - top_score[..., None])
    own_weight = jnp.exp(own_score - top_score)
    denom_sum = jnp.sum(weights, axis=-1) + own_weight
    accumulated = jnp.einsum(
        "rsn,rsnd->rsd", weights, key_data[..., head_dim:].astype(jnp.float32), precision=highest
    )
    accumulated = accumulated + own_weight[..., None] * value_full
    partial_value = (top_score, denom_sum, accumulated)
    pair_bit = lax.axis_size("tp").bit_length() - 2
    partial_value = join_pair(
        partial_value,
        from_partner((partial_value[0], partial_value[1], partial_value[2]), "tp", pair_bit),
    )
    attended = partial_value[2] / partial_value[1][..., None]
    first_half = halves[None, :, None] == 0
    attn_half = jnp.where(first_half, attended[..., :half_dim], attended[..., half_dim:])
    query_unit = unit_rows(query_full)
    key_unit = unit_rows(key_full)
    recalled = jnp.einsum("rsij,rsj->rsi", memory, query_unit, precision=highest)
    mixed_out = (attn_half + recalled).astype(jnp.bfloat16).reshape(req_count, -1)
    attn_term = jnp.dot(mixed_out, out_weight, preferred_element_type=jnp.float32)
    hidden_in = residual_in + lax.psum(attn_term, "tp")
    normed_mlp = rms_scale(hidden_in, norm_mlp).astype(jnp.bfloat16)
    gate_out = jnp.dot(normed_mlp, gate_weight, preferred_element_type=jnp.float32)
    up_out = jnp.dot(normed_mlp, up_weight, preferred_element_type=jnp.float32)
    activated = (jax.nn.silu(gate_out) * up_out).astype(jnp.bfloat16)
    rows_done = (
        hidden_in
        + lax.psum(
            jnp.dot(activated, down_weight, preferred_element_type=jnp.float32).astype(
                jnp.bfloat16
            ),
            "tp",
        ).astype(jnp.float32)
    ).astype(jnp.bfloat16)
    predicted = jnp.einsum("rsij,rsj->rsi", memory, key_unit, precision=highest)
    value_half = jnp.where(first_half, value_full[..., :half_dim], value_full[..., half_dim:])
    misfit = value_half - predicted
    keep_rate = forget[head_ids][None, :, None, None]
    step_rate = write_rate[head_ids][None, :, None, None]
    updated = keep_rate * memory + step_rate * misfit[..., None] * key_unit[:, :, None, :]
    mem_after = jnp.where(span_close[:, None, None, None] == 1, updated, memory)
    send_rows = rows_done[moved_slots].astype(jnp.float32)
    send_memory = mem_after[moved_slots].reshape(move_count, -1)
    dest_rows = lax.all_gather(move_dest[0], "rep", axis=0, tiled=True)
    out_part = lax.all_gather(send_rows.astype(jnp.bfloat16), "rep", axis=0, tiled=True).astype(
        jnp.float32
    )
    memory_rows = lax.all_gather(
        send_memory.astype(jnp.bfloat16), "rep", axis=0, tiled=True
    ).astype(jnp.float32)
    picked = picked_rows(dest_rows, my_rep, move_count)
    pick_full = picked.astype(jnp.float32).T
    rows_in = jnp.zeros(send_rows.shape, jnp.float32)
    memory_in = jnp.zeros(send_memory.shape, jnp.float32)
    rows_in = rows_in + jnp.dot(pick_full, out_part, precision=highest)
    memory_in = memory_in + jnp.dot(pick_full, memory_rows, precision=highest)
    rows_in, memory_in = (rows_in, memory_in)
    rows_done = rows_done.at[moved_slots].set(rows_in.astype(jnp.bfloat16))
    mem_after = mem_after.at[moved_slots].set(
        memory_in.reshape(move_count, sect_count, half_dim, head_dim)
    )
    return (rows_done, mem_after, new_pool)


def solution(mesh):
    placed = (
        P("rep", None),
        P("rep"),
        P("rep"),
        P("rep"),
        P("rep", None),
        P("rep", None),
        P("rep", None, None),
        P("rep", "tp", None, None),
        P(None, "tp", None, None),
        P("rep", "tp", None, None),
        P(),
        P(),
        P(None, "tp"),
        P("tp", None),
        P(None, "tp"),
        P(None, "tp"),
        P("tp", None),
        P(),
        P(),
    )
    return jax.shard_map(
        body,
        mesh=mesh,
        in_specs=placed,
        out_specs=(P("rep", None), P("rep", "tp", None, None), P("rep", "tp", None, None)),
        check_vma=False,
    )
```

profile of v0, /device:TPU:1, one launch (start us, length us, event | category | flops | bytes accessed | tf_op | source)
XLA Modules:
  0.0 315.0 jit_solution(13694322798186296017)
XLA Ops:
  8.1 1.3 copy.118
  9.8 29.9 %all-gather.2 = bf16[16,192,16]{1,2,0:T(8,128)(2,1)S(1)} all-gather(bf16[1,192,16]{1,2,0:T(8,128)(2,1)S(1)} %fusion.2), channel_id=1, replica_groups=mesh['rep'=32,'tp'=16] {'tp'}, dimensions={0}, use_global_device_ids=true | all-gather | bytes 104448 | tf_op jit(solution)/shard_map/all_gather | solution.py:98
  40.6 0.6 gather_fusion
  42.4 6.9 %collective-permute-start = (f32[16,1]{0,1:T(1,128)S(1)}, f32[16,1]{0,1:T(1,128)S(1)}, u32[]{:S(2)}, u32[]{:S(2)}) collective-permute-start(f32[16,1]{0,1:T(1,128)S(1)} %get-tuple-element.73), channel_id=1, source_target_pairs={{0,8},{8,0},{1,9},{9,1},{2,10},{10,2},{3,11},{11,3},{4,12},{12,4},... | collective-permute-start | bytes 200 | tf_op jit(solution)/shard_map/ppermute | solution.py:16
  49.4 7.1 %collective-permute-start.2 = (f32[16,1]{0,1:T(1,128)S(1)}, f32[16,1]{0,1:T(1,128)S(1)}, u32[]{:S(2)}, u32[]{:S(2)}) collective-permute-start(f32[16,1]{0,1:T(1,128)S(1)} %get-tuple-element.72), channel_id=1, source_target_pairs={{0,8},{8,0},{1,9},{9,1},{2,10},{10,2},{3,11},{11,3},{4,12},{12,4},... | collective-permute-start | bytes 200 | tf_op jit(solution)/shard_map/ppermute | solution.py:16
  56.5 0.7 fusion.6
  57.3 6.9 %collective-permute-start.1 = (f32[16,1,128]{2,0,1:T(8,128)S(1)}, f32[16,1,128]{2,0,1:T(8,128)S(1)}, u32[]{:S(2)}, u32[]{:S(2)}) collective-permute-start(f32[16,1,128]{2,0,1:T(8,128)S(1)} %fusion.59), channel_id=1, source_target_pairs={{0,8},{8,0},{1,9},{9,1},{2,10},{10,2},{3,11},{11,3},{4,12},{12,4},... | collective-permute-start | bytes 24584 | tf_op jit(solution)/shard_map/ppermute | solution.py:16
  64.9 0.7 dynamic-slice.20
  65.7 0.9 fusion.13
  66.6 0.9 fusion.15
  67.6 0.8 fusion.44
  68.4 1.0 fusion.12
  69.4 1.0 collective-permute-done.1
  70.5 0.8 fusion.53
  72.0 0.6 reshape.724
  72.7 0.6 gather_fusion.3
  73.9 0.7 reshape.726
  74.7 1.3 dynamic-slice.22
  76.7 22.4 %all-reduce.3 = s32[64]{0:T(128)S(1)} all-reduce(s32[64]{0:T(128)S(1)} %bitcast_dynamic-update-slice_fusion), channel_id=2, replica_groups=mesh['rep'=32,'tp'=16] {'rep'}, use_global_device_ids=true, to_apply=%add.3 | all-reduce | flops 64 | bytes 512
  99.1 101.1 %all-reduce.6.cloned.1.call-done = f32[16,1024]{1,0:T(8,128)} async-done(((f32[16,1024]{1,0:T(8,128)}), f32[16,1024]{1,0:T(8,128)}) %all-reduce.6.cloned.1.call-update) | async-done | bytes 65552 | tf_op jit(solution)/shard_map/psum | solution.py:156
  200.2 1.0 multiply_reduce_fusion
  201.2 0.9 multiply_convert_fusion
  202.8 39.7 %psum.15 = bf16[16,1024]{1,0:T(8,128)(2,1)S(1)} all-reduce(bf16[16,1024]{1,0:T(8,128)(2,1)S(1)} %convolution_convert_fusion.2), channel_id=1, replica_groups=mesh['rep'=32,'tp'=16] {'tp'}, use_global_device_ids=true, to_apply=%region_7.8 | all-reduce | flops 16384 | bytes 65536 | tf_op jit(solution)/shard_map/psum | solution.py:163
  242.5 0.9 add_convert_fusion
  243.9 48.1 %all-gather.3 = bf16[32,2,1024]{2,1,0:T(2,128)(2,1)S(1)} all-gather(bf16[1,2,1024]{2,1,0:T(2,128)(2,1)S(1)} %bitcast.202), channel_id=3, replica_groups=mesh['rep'=32,'tp'=16] {'rep'}, dimensions={0}, use_global_device_ids=true | all-gather | bytes 135168 | tf_op jit(solution)/shard_map/all_gather | solution.py:180
  292.3 0.7 scatter_fusion
  293.0 1.5 reshape.725
  294.9 0.6 scatter_fusion.1
  295.6 7.4 %reshape.727 = bf16[64,32768]{1,0:T(8,128)(2,1)} reshape(bf16[32,2,32768]{2,1,0:T(2,128)(2,1)} %all-gather.11.cloned.1.call-done) | data formatting | bytes 8388608
  303.0 3.0 convolution_convert_fusion
  306.0 0.6 scatter_fusion.2
  306.6 1.0 copy-done.1
  (104 shorter events, 6.8 us)
Async XLA Ops:
  8.0 1.6 copy-start
  8.0 1.5 copy-start.3
  8.0 32.0 %copy-start.14 = (s32[16]{0:T(128)S(1)}, s32[16]{0:T(128)}, u32[]{:S(2)}) copy-start(s32[16]{0:T(128)} %param.21) | copy-start | bytes 196
  8.0 1.4 copy-start.15
  8.0 31.9 %copy-start.9 = (bf16[8,1,64,256]{3,2,1,0:T(8,128)(2,1)S(1)}, bf16[8,1,64,256]{3,2,1,0:T(8,128)(2,1)}, u32[]{:S(2)}) copy-start(bf16[8,1,64,256]{3,2,1,0:T(8,128)(2,1)} %param.27) | copy-start | bytes 786436
  8.1 1.6 copy-start.11
  8.1 192.1 %all-reduce.6.cloned.1.call-start = ((), (), s32[]{:S(2)}) async-start(), calls=%async_computation | async-start | bytes 131072 | tf_op jit(solution)/shard_map/psum | solution.py:156
  40.4 0.8 copy-start.13
  41.5 22.8 %copy-start.16 = (f32[8]{0:T(128)S(1)}, f32[8]{0:T(128)}, u32[]{:S(2)}) copy-start(f32[8]{0:T(128)} %param.37) | copy-start | bytes 100
  41.5 23.4 %copy-start.17 = (f32[8]{0:T(128)S(1)}, f32[8]{0:T(128)}, u32[]{:S(2)}) copy-start(f32[8]{0:T(128)} %param.36) | copy-start | bytes 100
  41.5 24.1 %copy-start.18 = (s32[16]{0:T(128)S(1)}, s32[16]{0:T(128)}, u32[]{:S(2)}) copy-start(s32[16]{0:T(128)} %param.22) | copy-start | bytes 196
  41.5 24.2 %copy-start.2 = (f32[16,1,64,128]{3,2,1,0:T(8,128)S(1)}, f32[16,1,64,128]{3,2,1,0:T(8,128)}, u32[]{:S(2)}) copy-start(f32[16,1,64,128]{3,2,1,0:T(8,128)} %param.28) | copy-start | bytes 1572868
  42.4 26.9 %collective-permute-start = (f32[16,1]{0,1:T(1,128)S(1)}, f32[16,1]{0,1:T(1,128)S(1)}, u32[]{:S(2)}, u32[]{:S(2)}) collective-permute-start(f32[16,1]{0,1:T(1,128)S(1)} %get-tuple-element.73), channel_id=1, source_target_pairs={{0,8},{8,0},{1,9},{9,1},{2,10},{10,2},{3,11},{11,3},{4,12},{12,4},... | collective-permute-start | bytes 200 | tf_op jit(solution)/shard_map/ppermute | solution.py:16
  49.4 20.0 %collective-permute-start.2 = (f32[16,1]{0,1:T(1,128)S(1)}, f32[16,1]{0,1:T(1,128)S(1)}, u32[]{:S(2)}, u32[]{:S(2)}) collective-permute-start(f32[16,1]{0,1:T(1,128)S(1)} %get-tuple-element.72), channel_id=1, source_target_pairs={{0,8},{8,0},{1,9},{9,1},{2,10},{10,2},{3,11},{11,3},{4,12},{12,4},... | collective-permute-start | bytes 200 | tf_op jit(solution)/shard_map/ppermute | solution.py:16
  56.5 12.9 %copy-start.19 = (s32[1,2]{1,0:T(1,128)S(1)}, s32[1,2]{1,0:T(1,128)}, u32[]{:S(2)}) copy-start(s32[1,2]{1,0:T(1,128)} %param.23) | copy-start | bytes 28
  56.5 14.0 %copy-start.10 = (bf16[64,1024]{1,0:T(8,128)(2,1)S(1)}, bf16[64,1024]{1,0:T(8,128)(2,1)}, u32[]{:S(2)}) copy-start(bf16[64,1024]{1,0:T(8,128)(2,1)} %param.32) | copy-start | bytes 393220
  57.3 13.1 %collective-permute-start.1 = (f32[16,1,128]{2,0,1:T(8,128)S(1)}, f32[16,1,128]{2,0,1:T(8,128)S(1)}, u32[]{:S(2)}, u32[]{:S(2)}) collective-permute-start(f32[16,1,128]{2,0,1:T(8,128)S(1)} %fusion.59), channel_id=1, source_target_pairs={{0,8},{8,0},{1,9},{9,1},{2,10},{10,2},{3,11},{11,3},{4,12},{12,4},... | collective-permute-start | bytes 24584 | tf_op jit(solution)/shard_map/ppermute | solution.py:16
  66.6 10.0 %copy-start.20 = (s32[1,2]{1,0:T(1,128)S(1)}, s32[1,2]{1,0:T(1,128)}, u32[]{:S(2)}) copy-start(s32[1,2]{1,0:T(1,128)} %param.24) | copy-start | bytes 28
  67.6 133.6 %copy-start.12 = (f32[1024]{0:T(1024)S(1)}, f32[1024]{0:T(1024)}, u32[]{:S(2)}) copy-start(f32[1024]{0:T(1024)} %param.30) | copy-start | bytes 12292
  67.6 134.5 %copy-start.5 = (bf16[1024,176]{0,1:T(8,128)(2,1)S(1)}, bf16[1024,176]{0,1:T(8,128)(2,1)}, u32[]{:S(2)}) copy-start(bf16[1024,176]{0,1:T(8,128)(2,1)} %param.33) | copy-start | bytes 1081348
  68.4 133.9 %copy-start.6 = (bf16[176,1024]{1,0:T(8,128)(2,1)S(1)}, bf16[176,1024]{1,0:T(8,128)(2,1)}, u32[]{:S(2)}) copy-start(bf16[176,1024]{1,0:T(8,128)(2,1)} %param.35) | copy-start | bytes 1081348
  68.4 133.9 %copy-start.7 = (bf16[1024,176]{0,1:T(8,128)(2,1)S(1)}, bf16[1024,176]{0,1:T(8,128)(2,1)}, u32[]{:S(2)}) copy-start(bf16[1024,176]{0,1:T(8,128)(2,1)} %param.34) | copy-start | bytes 1081348
  71.4 221.7 %all-gather.9.cloned.1.call-start = ((), (), s32[]{:S(2)}) async-start(), calls=%async_computation.1 | async-start | bytes 1081344 | tf_op jit(solution)/shard_map/all_gather | solution.py:183
  72.6 222.9 %all-gather.11.cloned.1.call-start = ((), (), s32[]{:S(2)}) async-start(), calls=%async_computation.2 | async-start | bytes 4325376 | tf_op jit(solution)/shard_map/all_gather | solution.py:87
  293.0 1.9 copy-start.8
  295.5 7.5 %copy-start.4 = (f32[16,64,128]{2,1,0:T(8,128)}, f32[16,64,128]{2,1,0:T(8,128)S(1)}, u32[]{:S(2)}) copy-start(f32[16,64,128]{2,1,0:T(8,128)S(1)} %scatter_fusion.1) | copy-start | bytes 1572868
  306.6 1.0 copy-start.1
Sparse Core Ops, SparseCore 0:
  71.5 128.6 all-reduce.5
Sparse Core Ops, SparseCore 1:
  75.5 63.4 all-gather.8
  142.9 60.9 all-gather.10
where the time goes:
time: 316 us; the launch traced here: 315 us
  blocking collectives  140 us (44%)
  waiting for transfers between devices  102 us (32%)
  starting transfers between devices  21.1 us (7%)
  local copies, waits for them, and re-layouts  20.5 us (6%)
  between operations  16.7 us (5%)
  matrix products  8.74 us (3%)
  other arithmetic  5.7 us (2%)
    psum x1, waiting for transfers between devices, body(): hidden_in = residual_in + lax.psum(attn_term, 'tp')  101 us
    all_gather x1, blocking collectives, body(): lax.all_gather(send_rows.astype(jnp.bfloat16), 'rep', axis=0, tiled=True)  48.1 us
    psum x1, blocking collectives, body(): lax.psum(jnp.dot(activated, down_weight, preferred_element_type=jnp.float...  39.7 us
    all_gather x1, blocking collectives, body(): qkv_full = lax.all_gather(qkv_part, 'tp', axis=1, tiled=True)  29.9 us
    unnamed x1, blocking collectives  22.4 us
    ppermute x3, starting transfers between devices, from_partner(): return lax.ppermute(block, axis, route)  20.9 us
    unnamed x58, local copies, waits for them, and re-layouts  14.2 us
  transfers between devices with their start and end apart: 6, of which 2 were waited for; matrix products, arithmetic and copies ran while one was open for 6% of the time, Pallas kernels for 0%

commit v1 on v0

v1 whole, which is shorter than its diff:
```python
import jax
import jax.numpy as jnp
from jax import lax
from jax.experimental import pallas as pl
from jax.experimental.pallas import tpu as pltpu
from jax.sharding import PartitionSpec as P

f32 = jnp.float32
bf16 = jnp.bfloat16
highest = lax.Precision.HIGHEST
LANES = 128

VMEM = pl.BlockSpec(memory_space=pltpu.VMEM)
SMEM = pl.BlockSpec(memory_space=pltpu.SMEM)
HBM = pl.BlockSpec(memory_space=pl.ANY)


def call(kernel, outs, in_specs, out_specs=None, scratch=(), aliases=None):
    return pl.pallas_call(
        kernel,
        out_shape=outs,
        in_specs=in_specs,
        out_specs=out_specs if out_specs is not None else jax.tree.map(lambda _: VMEM, outs),
        scratch_shapes=scratch,
        input_output_aliases=aliases or {},
        compiler_params=pltpu.CompilerParams(vmem_limit_bytes=48 << 20),
    )


def lane_ids(shape):
    return lax.broadcasted_iota(jnp.int32, shape, len(shape) - 1)


def row_ids(shape):
    return lax.broadcasted_iota(jnp.int32, shape, len(shape) - 2)


def column(values, count, lanes=LANES):
    rows = row_ids((count, lanes))
    out = jnp.zeros((count, lanes), jnp.int32)
    for r in range(count):
        out = jnp.where(rows == r, values[r], out)
    return out


def half_swap(block):
    return pltpu.roll(block, LANES // 2, 1)


def qkv_kernel(tokens, gain, weight, out):
    t = lax.axis_index("tp")
    x = tokens[...].astype(f32)
    scale = lax.rsqrt(jnp.mean(x * x, axis=-1, keepdims=True) + 1e-05)
    normed = (x * scale * gain[...]).astype(bf16)
    part = jnp.dot(normed, weight[...], preferred_element_type=f32)
    part = part.astype(bf16).astype(f32)
    first = part[:, :LANES]
    last = part[:, LANES:]
    turned = half_swap(first)
    lanes = lane_ids(first.shape)
    low = lanes < 64
    blocks = (
        jnp.where(low, first, turned),
        jnp.where(low, turned, first),
        jnp.concatenate([last, last], axis=1),
    )
    placed = []
    for j, block in enumerate(blocks):
        sub = lax.rem(3 * t + j, 2)
        placed.append(jnp.where(lanes // 64 == sub, block, 0.0))
    for head in range(8):
        slot = jnp.zeros(first.shape, f32)
        for j in range(3):
            mine = lax.rem(3 * t + j, 16) // 2 == head
            slot = slot + jnp.where(mine, placed[j], 0.0)
        out[head] = slot.astype(bf16)
        out[head + 8] = slot.astype(bf16)


def attend_kernel(
    lengths, groups, span, pages, slots, forget, rate,
    recv, pool, prefix, memory, own_weight, pair_weight,
    terms_out, memory_out, send_out,
    masked, terms,
):
    t = lax.axis_index("tp")
    half = t // 8
    head = lax.rem(t, 8)

    def pick(kind):
        one = (16 * kind + 2 * head) // 3
        two = (16 * kind + 2 * head + 1) // 3
        a = recv[one].astype(f32)
        b = recv[two].astype(f32)
        return jnp.where(one == two, a, a + b)

    query = pick(0)
    key = pick(1)
    value = pick(2)
    rows = query.shape[0]
    shape = (rows, LANES)
    lanes = lane_ids(shape)
    row = row_ids(shape)
    low = lanes < 64
    length = column(lengths, rows)
    group = column(groups, rows)
    page = jnp.zeros(shape, jnp.int32)
    for r in range(rows):
        page = jnp.where(row == r, pages[2 * r + half], page)

    score_scale = LANES ** (-0.5)
    nt = (((1,), (1,)), ((), ()))
    page_count = pool.shape[0]
    query_b = query.astype(bf16)
    pool_keys = pool[:, :, :LANES].reshape(page_count * LANES, LANES)
    pool_scores = lax.dot_general(query_b, pool_keys, nt, preferred_element_type=f32)
    pre_rows = prefix.shape[0] * prefix.shape[1]
    pre_keys = prefix[:, :, :LANES].reshape(pre_rows, LANES)
    pre_scores = lax.dot_general(query_b, pre_keys, nt, preferred_element_type=f32)
    tiles = []
    in_reach = lanes + half * LANES < length
    for p in range(page_count):
        live = (page == p) & in_reach
        tile = pool_scores[:, p * LANES : (p + 1) * LANES] * score_scale
        tiles.append(jnp.where(live, tile, -jnp.inf))
    for p in range(pre_rows // LANES):
        live = group == lanes // 64 + 2 * p
        tile = pre_scores[:, p * LANES : (p + 1) * LANES] * score_scale
        tiles.append(jnp.where(live, tile, -jnp.inf))
    own = jnp.sum(query * key, axis=-1, keepdims=True) * score_scale
    own = jnp.where(half == 0, own, -jnp.inf)
    peak = tiles[0]
    for tile in tiles[1:]:
        peak = jnp.maximum(peak, tile)
    top = jnp.maximum(jnp.max(peak, axis=-1, keepdims=True), own)
    weights = [jnp.exp(tile - top) for tile in tiles]
    own_weight_ = jnp.exp(own - top)
    total = weights[0]
    for tile in weights[1:]:
        total = total + tile
    denom = jnp.sum(total, axis=-1, keepdims=True) + own_weight_

    def both(parts):
        full = jnp.concatenate(parts, axis=1)
        upper = full.astype(bf16)
        lower = (full - upper.astype(f32)).astype(bf16)
        return jnp.concatenate([upper, lower], axis=0)

    pool_values = pool[:, :, LANES:].reshape(page_count * LANES, LANES)
    pre_values = prefix[:, :, LANES:].reshape(pre_rows, LANES)
    summed = jnp.dot(both(weights[:page_count]), pool_values, preferred_element_type=f32)
    summed = summed + jnp.dot(
        both(weights[page_count:]), pre_values, preferred_element_type=f32
    )
    summed = summed[:rows] + summed[rows:] + own_weight_ * value
    attended = summed / denom
    lse = top + jnp.log(denom)

    query_unit = query * lax.rsqrt(jnp.sum(query * query, axis=-1, keepdims=True) + 1e-06)
    key_unit = key * lax.rsqrt(jnp.sum(key * key, axis=-1, keepdims=True) + 1e-06)
    mem_rows = memory.shape[1]
    flat_memory = memory[...].reshape(rows * mem_rows, LANES)
    seen = lax.dot_general(
        jnp.concatenate([query_unit, key_unit], axis=0), flat_memory, nt,
        preferred_element_type=f32, precision=highest,
    )
    recalled = jnp.zeros(shape, f32)
    value_half = jnp.where(half == 0, value, half_swap(value))
    value_both = jnp.where(low, value_half, half_swap(value_half))
    closing = column(span, rows) == 1
    step = rate[head]
    keep = forget[head]
    for c in range(rows // 2):
        mine = row == 2 * c + lanes // 64
        cut = slice(c * LANES, (c + 1) * LANES)
        recalled = recalled + jnp.where(mine, seen[:rows, cut], 0.0)
        misfit = (value_both - seen[rows:, cut]) * step
        masked[:, cut] = jnp.where(mine & closing, misfit, 0.0)
    recalled = recalled + half_swap(recalled)
    change = lax.dot_general(
        masked[...], key_unit, (((0,), (0,)), ((), ())),
        preferred_element_type=f32, precision=highest,
    )
    for r in range(rows):
        decay = jnp.where(span[r] == 1, keep, 1.0)
        memory_out[r] = decay * memory[r] + change[r * mem_rows : (r + 1) * mem_rows]

    for m in range(2):
        slot = slots[0, m]
        send_out[m * LANES : (m + 1) * LANES, :] = pool[pages[2 * slot + half]]
        send_out[2 * LANES :, m * LANES : (m + 1) * LANES] = memory_out[slot].astype(bf16)

    turned = jnp.where(half == 0, attended, half_swap(attended))
    left = jnp.concatenate([turned, jnp.where(low, recalled, 0.0)], axis=0).astype(bf16)
    right = jnp.concatenate([own_weight[...], pair_weight[...]], axis=0)
    projected = jnp.dot(left, right, preferred_element_type=f32)
    for k in range(8):
        terms[:, k, :] = projected[:rows, k * LANES : (k + 1) * LANES]
        terms[:, k + 8, :] = projected[rows:, k * LANES : (k + 1) * LANES]
    one = lse.astype(bf16).astype(f32)
    two = (lse - one).astype(bf16).astype(f32)
    terms[:, 16, :] = jnp.broadcast_to(one, shape)
    terms[:, 17, :] = jnp.broadcast_to(two, shape)
    terms[:, 18, :] = jnp.broadcast_to(lse - one - two, shape)
    for k in range(19, 24):
        terms[:, k, :] = jnp.zeros(shape, f32)
    terms_out[...] = terms[...].astype(bf16)


def hidden_kernel(recv, tokens, gain, hidden_out, normed_out, terms):
    t = lax.axis_index("tp")
    terms[...] = recv[...].astype(f32)
    lse = terms[:, 16, :] + terms[:, 17, :] + terms[:, 18, :]
    count = lse.shape[0]
    other = jnp.concatenate([lse[count // 2 :], lse[: count // 2]], axis=0)
    share = 1.0 / (1.0 + jnp.exp(other - lse))
    x = tokens[...].astype(f32)
    x = jnp.sum(jnp.where(row_ids(x.shape) == t, x, 0.0), axis=0, keepdims=True)
    parts = []
    for k in range(8):
        part = share * terms[:, k, :] + terms[:, k + 8, :]
        part = jnp.sum(part, axis=0, keepdims=True)
        parts.append(part + x[:, k * LANES : (k + 1) * LANES])
    hidden = jnp.concatenate(parts, axis=0)
    hidden_out[...] = hidden
    square = jnp.sum(jnp.sum(hidden * hidden, axis=1, keepdims=True), axis=0, keepdims=True)
    scale = lax.rsqrt(square / (8 * LANES) + 1e-05)
    normed = (hidden * scale * gain[...]).astype(bf16)
    for s in range(16):
        normed_out[s] = normed


def mlp_kernel(recv, gate_weight, up_weight, down_weight, out, rows):
    rows[...] = recv[...].astype(f32)
    x = jnp.concatenate([rows[:, k, :] for k in range(8)], axis=1).astype(bf16)
    gate = jnp.dot(x, gate_weight[...], preferred_element_type=f32)
    up = jnp.dot(x, up_weight[...], preferred_element_type=f32)
    active = (gate * (1.0 / (1.0 + jnp.exp(-gate))) * up).astype(bf16)
    y = jnp.dot(active, down_weight[...], preferred_element_type=f32)
    for k in range(8):
        rows[:, k, :] = y[:, k * LANES : (k + 1) * LANES]
    out[...] = rows[...].astype(bf16)


def row_kernel(recv, hidden, out):
    total = hidden[...]
    for s in range(recv.shape[0]):
        total = total + recv[s].astype(f32)
    row = total.astype(bf16)
    for s in range(16):
        out[s] = row


def leave_kernel(slots, dests, recv, out):
    shape = (8, LANES)
    code = jnp.where(row_ids(shape) == 0, dests[0, 0], dests[0, 1]).astype(f32).astype(bf16)
    for s in range(out.shape[0]):
        out[s, 0:8, :] = recv[slots[0, 0]]
        out[s, 8:16, :] = recv[slots[0, 1]]
        out[s, 16:24, :] = code


def finish_kernel(
    pages, slots, rows_all, recv, pool, gathered, memory,
    rows_out, pool_out, memory_out,
    codes, rows, raw, wide, pool_sem, page_sem, raw_sem, wide_sem,
):
    t = lax.axis_index("tp")
    me = lax.axis_index("rep")
    half = t // 8
    sources = recv.shape[0]
    codes[...] = recv[:, 16:24, :].astype(f32)
    shape = (sources, LANES)
    row = row_ids(shape)
    base = [
        pltpu.make_async_copy(pool.at[p], pool_out.at[p], pool_sem.at[p])
        for p in range(pool.shape[0])
    ]
    taken = [pages[2 * slots[0, m] + half] for m in range(2)]
    for p, copy in enumerate(base):

        @pl.when((taken[0] != p) & (taken[1] != p))
        def _(copy=copy):
            copy.start()

    moved = []
    for m in range(2):
        match = codes[:, m, :] == me.astype(f32)
        source = jnp.max(jnp.where(match, row, 0))
        page_in = pltpu.make_async_copy(
            gathered.at[source, pl.ds(m * LANES, LANES), :], pool_out.at[taken[m]], page_sem.at[m]
        )
        raw_in = pltpu.make_async_copy(
            gathered.at[source, pl.ds(2 * LANES, 64), :], raw.at[m], raw_sem.at[m]
        )
        page_in.start()
        raw_in.start()
        moved.append((page_in, raw_in, source))
    rows[...] = rows_all[...].astype(f32)
    for m in range(2):
        rows[slots[0, m]] = recv[moved[m][2], 8 * m : 8 * m + 8, :].astype(f32)
    for k in range(8):
        rows_out[:, k * LANES : (k + 1) * LANES] = rows[:, k, :].astype(bf16)
    for m in range(2):
        moved[m][1].wait()
        wide[m] = raw[m, :, m * LANES : (m + 1) * LANES].astype(f32)
        pltpu.make_async_copy(wide.at[m], memory_out.at[slots[0, m]], wide_sem.at[m]).start()
    for m in range(2):
        pltpu.make_async_copy(wide.at[m], memory_out.at[slots[0, m]], wide_sem.at[m]).wait()
        moved[m][0].wait()
    for p, copy in enumerate(base):

        @pl.when((taken[0] != p) & (taken[1] != p))
        def _(copy=copy):
            copy.wait()


def body(
    tokens,
    lengths,
    prompt_group,
    span_close,
    out_slot,
    move_dest,
    page_table,
    cache_pool,
    prefix_cache,
    memory,
    norm_attn,
    norm_mlp,
    qkv_weight,
    out_weight,
    gate_weight,
    up_weight,
    down_weight,
    forget,
    write_rate,
):
    shape = jax.ShapeDtypeStruct
    rows = tokens.shape[0]
    n_tp = lax.axis_size("tp")
    n_rep = lax.axis_size("rep")
    pages = page_table.reshape(-1)
    pool = cache_pool[:, 0]
    prefix = prefix_cache[:, 0]
    mem = memory[:, 0]
    pair_weight = lax.ppermute(
        out_weight, "tp", [(i, (i + n_tp // 2) % n_tp) for i in range(n_tp)]
    )

    qkv_slots = call(
        qkv_kernel, shape((n_tp, rows, LANES), bf16), [VMEM] * 3
    )(tokens, norm_attn.reshape(1, -1), qkv_weight)
    qkv_recv = lax.all_to_all(qkv_slots, "tp", 0, 0)

    terms, mem_after, send = call(
        attend_kernel,
        (
            shape((n_tp, 24, LANES), bf16),
            shape(mem.shape, f32),
            shape((2 * LANES + 64, 2 * LANES), bf16),
        ),
        [SMEM] * 7 + [VMEM] * 6,
        scratch=[pltpu.VMEM((rows, rows * 64), f32), pltpu.VMEM((rows, 24, LANES), f32)],
    )(
        lengths, prompt_group, span_close, pages, out_slot, forget, write_rate,
        qkv_recv, pool, prefix, mem, out_weight, pair_weight,
    )
    gathered = lax.all_gather(send, "rep", axis=0)
    terms_recv = lax.all_to_all(terms, "tp", 0, 0)

    hidden, normed_slots = call(
        hidden_kernel,
        (shape((8, LANES), f32), shape((n_tp, 8, LANES), bf16)),
        [VMEM] * 3,
        scratch=[pltpu.VMEM((n_tp, 24, LANES), f32)],
    )(terms_recv, tokens, norm_mlp.reshape(8, LANES))
    normed_recv = lax.all_to_all(normed_slots, "tp", 0, 0)

    down_slots = call(
        mlp_kernel,
        shape((n_tp, 8, LANES), bf16),
        [VMEM] * 4,
        scratch=[pltpu.VMEM((rows, 8, LANES), f32)],
    )(normed_recv, gate_weight, up_weight, down_weight)
    down_recv = lax.all_to_all(down_slots, "tp", 0, 0)

    row_slots = call(row_kernel, shape((n_tp, 8, LANES), bf16), [VMEM] * 2)(down_recv, hidden)
    rows_all = lax.all_to_all(row_slots, "tp", 0, 0)

    leaving = call(
        leave_kernel, shape((n_rep, 24, LANES), bf16), [SMEM, SMEM, VMEM]
    )(out_slot, move_dest, rows_all)
    arrived = lax.all_to_all(leaving, "rep", 0, 0)

    rows_out, pool_out, mem_out = call(
        finish_kernel,
        (shape(tokens.shape, bf16), shape(pool.shape, bf16), shape(mem.shape, f32)),
        [SMEM, SMEM, VMEM, VMEM, HBM, HBM, HBM],
        out_specs=(VMEM, HBM, HBM),
        scratch=[
            pltpu.VMEM((n_rep, 8, LANES), f32),
            pltpu.VMEM((rows, 8, LANES), f32),
            pltpu.VMEM((2, 64, 2 * LANES), bf16),
            pltpu.VMEM((2, 64, LANES), f32),
            pltpu.SemaphoreType.DMA((pool.shape[0],)),
            pltpu.SemaphoreType.DMA((2,)),
            pltpu.SemaphoreType.DMA((2,)),
            pltpu.SemaphoreType.DMA((2,)),
        ],
        aliases={6: 2},
    )(pages, out_slot, rows_all, arrived, pool, gathered, mem_after)
    return rows_out, mem_out[:, None], pool_out[:, None]


def solution(mesh):
    placed = (
        P("rep", None),
        P("rep"),
        P("rep"),
        P("rep"),
        P("rep", None),
        P("rep", None),
        P("rep", None, None),
        P("rep", "tp", None, None),
        P(None, "tp", None, None),
        P("rep", "tp", None, None),
        P(),
        P(),
        P(None, "tp"),
        P("tp", None),
        P(None, "tp"),
        P(None, "tp"),
        P("tp", None),
        P(),
        P(),
    )
    return jax.shard_map(
        body,
        mesh=mesh,
        in_specs=placed,
        out_specs=(P("rep", None), P("rep", "tp", None, None), P("rep", "tp", None, None)),
        check_vma=False,
    )
```

time: 316 us -> 166 us (0.53)
  waiting for transfers between devices: 102 us -> 12.6 us
  blocking collectives: 140 us -> 78.9 us
  Pallas kernels: 0 us -> 12.6 us
  starting transfers between devices: 21.1 us -> 31.3 us
  matrix products: 8.74 us -> 0 us
  other arithmetic: 5.7 us -> 0 us
  local copies, waits for them, and re-layouts: 20.5 us -> 15.5 us
    psum x1 -> x0, waiting for transfers between devices: 101 us -> none  [body(): hidden_in = residual_in + lax.psum(attn_term, 'tp')]
    all_to_all x0 -> x4, blocking collectives: none -> 78.9 us  [the longest x1 28.4 us: body(): terms_recv = lax.all_to_all(terms, 'tp', 0, 0)]
    all_gather x2 -> x0, blocking collectives: 78 us -> none  [the longest x1 48.1 us: body(): lax.all_gather(send_rows.astype(jnp.bfloat16), 'rep', axis=0, tiled=True)]
    psum x1 -> x0, blocking collectives: 39.7 us -> none  [body(): lax.psum(jnp.dot(activated, down_weight, preferred_element_type=jnp.float...]
    unnamed x1 -> x0, blocking collectives: 22.4 us -> none
    all_to_all x0 -> x2, starting transfers between devices: none -> 19.2 us  [the longest x1 15.7 us: body(): qkv_recv = lax.all_to_all(qkv_slots, 'tp', 0, 0)]
    pallas_call x0 -> x7, Pallas kernels: none -> 12.6 us  [the longest x1 6.68 us: body(): call(finish_kernel, (shape(tokens.shape, bf16), shape(pool.shape, bf16),...]
    all_to_all x0 -> x2, waiting for transfers between devices: none -> 9.02 us  [the longest x1 9.02 us: body(): normed_recv = lax.all_to_all(normed_slots, 'tp', 0, 0)]
  transfers between devices with their start and end apart: 6 -> 4, of which waited for: 2 -> 2; matrix products, arithmetic and copies ran while one was open for 6% -> 2% of each run, Pallas kernels for 0% -> 1%
where the time goes in v1:
time: 166 us; the launch traced here: 165 us
  blocking collectives  78.9 us (48%)
  starting transfers between devices  31.3 us (19%)
  local copies, waits for them, and re-layouts  15.5 us (9%)
  between operations  14.1 us (8%)
  Pallas kernels  12.6 us (8%)
  waiting for transfers between devices  12.6 us (8%)
    all_to_all x1, blocking collectives, body(): terms_recv = lax.all_to_all(terms, 'tp', 0, 0)  28.4 us
    all_to_all x1, blocking collectives, body(): arrived = lax.all_to_all(leaving, 'rep', 0, 0)  22.6 us
    all_to_all x1, starting transfers between devices, body(): qkv_recv = lax.all_to_all(qkv_slots, 'tp', 0, 0)  15.7 us
    unnamed x40, local copies, waits for them, and re-layouts  15.4 us
    all_to_all x1, blocking collectives, body(): down_recv = lax.all_to_all(down_slots, 'tp', 0, 0)  14 us
    all_to_all x1, blocking collectives, body(): rows_all = lax.all_to_all(row_slots, 'tp', 0, 0)  14 us
    ppermute x1, starting transfers between devices, body(): lax.ppermute(out_weight, 'tp', [(i, (i + n_tp // 2) % n_tp) for i in rang...  12 us
    all_to_all x1, waiting for transfers between devices, body(): normed_recv = lax.all_to_all(normed_slots, 'tp', 0, 0)  9.02 us
  transfers between devices with their start and end apart: 4, of which 2 were waited for; matrix products, arithmetic and copies ran while one was open for 2% of the time, Pallas kernels for 1%

profile of v1, /device:TPU:1, one launch (start us, length us, event | category | flops | bytes accessed | tf_op | source)
XLA Modules:
  0.0 165.0 jit_solution(2210827645742929920)
XLA Ops:
  7.2 1.3 copy.30.weight
  8.5 0.7 copy-done.6
  9.3 0.7 copy-done.10
  9.9 1.0 shard_map.202
  10.9 15.7 %all-to-all-start = ((bf16[16,16,128]{2,1,0:T(8,128)(2,1)}), bf16[16,16,128]{2,1,0:T(8,128)(2,1)S(1)}, u32[]{:S(2)}, u32[]{:S(2)}) async-start(bf16[16,16,128]{2,1,0:T(8,128)(2,1)} %shard_map.202), calls=%async_computation | async-start | bytes 131072 | tf_op jit(solution)/shard_map/all_to_all | solution.py:354
  26.7 12.0 %collective-permute-start = (bf16[64,1024]{1,0:T(8,128)(2,1)}, bf16[64,1024]{1,0:T(8,128)(2,1)S(1)}, u32[]{:S(2)}, u32[]{:S(2)}) collective-permute-start(bf16[64,1024]{1,0:T(8,128)(2,1)} %own_weight.1), channel_id=1, source_target_pairs={{0,8},{1,9},{2,10},{3,11},{4,12},{5,13},{6,14},{7,15},{8,0},{9,1},... | collective-permute-start | bytes 393224 | tf_op jit(solution)/shard_map/ppermute | solution.py:347
  38.7 0.8 copy.29
  39.6 3.6 %collective-permute-done.pair_weight = bf16[64,1024]{1,0:T(8,128)(2,1)S(1)} collective-permute-done((bf16[64,1024]{1,0:T(8,128)(2,1)}, bf16[64,1024]{1,0:T(8,128)(2,1)S(1)}, u32[]{:S(2)}, u32[]{:S(2)}) %collective-permute-start) | collective-permute-done | bytes 131104 | tf_op jit(solution)/shard_map/ppermute | solution.py:347
  43.1 1.2 copy-done
  44.4 1.0 copy-done.2
  45.4 0.9 copy-done.4
  46.3 0.9 copy-done.5
  47.3 0.7 copy-done.8
  47.9 0.7 copy-done.12
  48.6 0.7 copy-done.13
  49.2 0.7 copy-done.14
  49.9 0.7 copy-done.15
  50.5 0.7 copy-done.16
  51.2 3.1 %shard_map.203 = (bf16[16,24,128]{2,1,0:T(8,128)(2,1)S(1)}, f32[16,64,128]{2,1,0:T(8,128)}, bf16[320,256]{1,0:T(8,128)(2,1)}) custom-call(s32[16]{0:T(128)S(1)} %copy-done.12, s32[16]{0:T(128)S(1)} %copy-done.13, s32[16]{0:T(128)S(1)} %copy-done.14, s32[32]{0:T(128)S(1)} %reshape.15.pages, s32[1,2]{1,0:T(1,128)S(1)} %copy-done.8, f32[8]{0:T(128)S(1)} %copy-done.15, ...), custom_call_target="tpu_custom_call" | custom-call | tf_op jit(solution)/shard_map/pallas_call | solution.py:356
  54.3 28.4 %all_to_all.30.recv = bf16[16,24,128]{2,1,0:T(8,128)(2,1)S(1)} all-to-all(bf16[16,24,128]{2,1,0:T(8,128)(2,1)S(1)} %get-tuple-element.11), channel_id=1, replica_groups=mesh['rep'=32,'tp'=16] {'tp'}, dimensions={0} | all-to-all | bytes 196608 | tf_op jit(solution)/shard_map/all_to_all | solution.py:370
  82.7 0.8 copy-done.7
  83.5 0.7 copy-done.11
  84.1 0.8 shard_map.204
  85.0 3.5 %all-to-all-start.2 = ((bf16[16,8,128]{2,1,0:T(8,128)(2,1)}), bf16[16,8,128]{2,1,0:T(8,128)(2,1)S(1)}, u32[]{:S(2)}, u32[]{:S(2)}) async-start(bf16[16,8,128]{2,1,0:T(8,128)(2,1)} %get-tuple-element.12), calls=%async_computation.2 | async-start | bytes 65536 | tf_op jit(solution)/shard_map/all_to_all | solution.py:378
  88.5 1.2 copy.31.gate_weight
  89.7 1.2 copy.32.up_weight
  90.9 9.0 %all-to-all-done.2.recv = bf16[16,8,128]{2,1,0:T(8,128)(2,1)S(1)} async-done(((bf16[16,8,128]{2,1,0:T(8,128)(2,1)}), bf16[16,8,128]{2,1,0:T(8,128)(2,1)S(1)}, u32[]{:S(2)}, u32[]{:S(2)}) %all-to-all-start.2) | async-done | bytes 32800 | tf_op jit(solution)/shard_map/all_to_all | solution.py:378
  100.3 14.0 %all_to_all.31.recv = bf16[16,8,128]{2,1,0:T(8,128)(2,1)S(1)} all-to-all(bf16[16,8,128]{2,1,0:T(8,128)(2,1)S(1)} %shard_map.205), channel_id=1, replica_groups=mesh['rep'=32,'tp'=16] {'tp'}, dimensions={0} | all-to-all | bytes 65536 | tf_op jit(solution)/shard_map/all_to_all | solution.py:386
  114.3 14.0 %all_to_all.32.recv.rows_all = bf16[16,8,128]{2,1,0:T(8,128)(2,1)S(1)} all-to-all(bf16[16,8,128]{2,1,0:T(8,128)(2,1)S(1)} %shard_map.206), channel_id=1, replica_groups=mesh['rep'=32,'tp'=16] {'tp'}, dimensions={0} | all-to-all | bytes 65536 | tf_op jit(solution)/shard_map/all_to_all | solution.py:389
  128.3 0.6 shard_map.207
  128.9 22.6 %all_to_all.33.recv = bf16[32,24,128]{2,1,0:T(8,128)(2,1)S(1)} all-to-all(bf16[32,24,128]{2,1,0:T(8,128)(2,1)S(1)} %shard_map.207), channel_id=1, replica_groups=mesh['rep'=32,'tp'=16] {'rep'}, dimensions={0} | all-to-all | bytes 393216 | tf_op jit(solution)/shard_map/all_to_all | solution.py:394
  151.4 6.7 %shard_map.208 = (bf16[16,1024]{1,0:T(8,128)(2,1)}, bf16[16,128,256]{2,1,0:T(8,128)(2,1)}, f32[16,64,128]{2,1,0:T(8,128)}) custom-call(s32[32]{0:T(128)S(1)} %reshape.15.pages, s32[1,2]{1,0:T(1,128)S(1)} %copy-done.9, bf16[16,8,128]{2,1,0:T(8,128)(2,1)S(1)} %all_to_all.32.recv.rows_all, ...), custom_call_target="tpu_custom_call", output_to_operand_aliasing={{2}: (6, {})} | custom-call | tf_op jit(solution)/shard_map/pallas_call | solution.py:396
  (29 shorter events, 0.6 us)
Async XLA Ops:
  7.2 144.3 %copy-start.1 = (bf16[16,1,128,256]{3,2,1,0:T(8,128)(2,1)S(1)}, bf16[16,1,128,256]{3,2,1,0:T(8,128)(2,1)}, u32[]{:S(2)}) copy-start(bf16[16,1,128,256]{3,2,1,0:T(8,128)(2,1)} %param.26) | copy-start | bytes 3145732
  7.2 92.7 %copy-start.3 = (bf16[176,1024]{1,0:T(8,128)(2,1)S(1)}, bf16[176,1024]{1,0:T(8,128)(2,1)}, u32[]{:S(2)}) copy-start(bf16[176,1024]{1,0:T(8,128)(2,1)} %down_weight.1) | copy-start | bytes 1081348
  8.5 0.8 copy-start.6
  9.3 0.7 copy-start.10
  9.9 118.3 %copy-start.9 = (s32[1,2]{1,0:T(1,128)S(1)}, s32[1,2]{1,0:T(1,128)}, u32[]{:S(2)}) copy-start(s32[1,2]{1,0:T(1,128)} %slots.5) | copy-start | bytes 28
  9.9 118.3 %copy-start.17 = (s32[1,2]{1,0:T(1,128)S(1)}, s32[1,2]{1,0:T(1,128)}, u32[]{:S(2)}) copy-start(s32[1,2]{1,0:T(1,128)} %dests.1) | copy-start | bytes 28
  10.9 32.2 %all-to-all-start = ((bf16[16,16,128]{2,1,0:T(8,128)(2,1)}), bf16[16,16,128]{2,1,0:T(8,128)(2,1)S(1)}, u32[]{:S(2)}, u32[]{:S(2)}) async-start(bf16[16,16,128]{2,1,0:T(8,128)(2,1)} %shard_map.202), calls=%async_computation | async-start | bytes 131072 | tf_op jit(solution)/shard_map/all_to_all | solution.py:354
  26.7 124.8 %all-gather.3.cloned.1.call-start = ((), (), s32[]{:S(2)}) async-start(), calls=%async_computation.6 | async-start | bytes 5406720 | tf_op jit(solution)/shard_map/all_gather | solution.py:369
  26.7 16.4 %collective-permute-start = (bf16[64,1024]{1,0:T(8,128)(2,1)}, bf16[64,1024]{1,0:T(8,128)(2,1)S(1)}, u32[]{:S(2)}, u32[]{:S(2)}) collective-permute-start(bf16[64,1024]{1,0:T(8,128)(2,1)} %own_weight.1), channel_id=1, source_target_pairs={{0,8},{1,9},{2,10},{3,11},{4,12},{5,13},{6,14},{7,15},{8,0},{9,1},... | collective-permute-start | bytes 393224 | tf_op jit(solution)/shard_map/ppermute | solution.py:347
  43.1 1.2 copy-start
  44.4 1.0 copy-start.2
  45.4 0.9 copy-start.4
  46.3 0.9 copy-start.5
  47.2 0.7 copy-start.8
  47.9 0.7 copy-start.12
  48.6 0.7 copy-start.13
  49.2 0.7 copy-start.14
  49.9 0.7 copy-start.15
  50.5 0.7 copy-start.16
  82.7 0.8 copy-start.7
  83.4 0.7 copy-start.11
  85.0 14.9 %all-to-all-start.2 = ((bf16[16,8,128]{2,1,0:T(8,128)(2,1)}), bf16[16,8,128]{2,1,0:T(8,128)(2,1)S(1)}, u32[]{:S(2)}, u32[]{:S(2)}) async-start(bf16[16,8,128]{2,1,0:T(8,128)(2,1)} %get-tuple-element.12), calls=%async_computation.2 | async-start | bytes 65536 | tf_op jit(solution)/shard_map/all_to_all | solution.py:378
Sparse Core Ops, SparseCore 0:
  54.4 71.0 all-gather.2

commit v2 on v1

v2 whole, which is shorter than its diff:
```python
import jax
import jax.numpy as jnp
from jax import lax
from jax.experimental import pallas as pl
from jax.experimental.pallas import tpu as pltpu
from jax.sharding import PartitionSpec as P

f32 = jnp.float32
bf16 = jnp.bfloat16
highest = lax.Precision.HIGHEST
LANES = 128
NT = (((1,), (1,)), ((), ()))

VMEM = pl.BlockSpec(memory_space=pltpu.VMEM)
SMEM = pl.BlockSpec(memory_space=pltpu.SMEM)
HBM = pl.BlockSpec(memory_space=pltpu.MemorySpace.HBM)


def call(kernel, outs, in_specs, out_specs=None, scratch=(), aliases=None):
    return pl.pallas_call(
        kernel,
        out_shape=outs,
        in_specs=in_specs,
        out_specs=out_specs if out_specs is not None else jax.tree.map(lambda _: VMEM, outs),
        scratch_shapes=scratch,
        input_output_aliases=aliases or {},
        compiler_params=pltpu.CompilerParams(vmem_limit_bytes=24 << 20),
    )


def in_hbm(*arrays):
    return [pltpu.with_memory_space_constraint(a, pltpu.MemorySpace.HBM) for a in arrays]


def lane_ids(shape):
    return lax.broadcasted_iota(jnp.int32, shape, len(shape) - 1)


def row_ids(shape):
    return lax.broadcasted_iota(jnp.int32, shape, len(shape) - 2)


def column(read, count):
    rows = row_ids((count, LANES))
    out = jnp.zeros((count, LANES), jnp.int32)
    for r in range(count):
        out = jnp.where(rows == r, read(r), out)
    return out


def half_swap(block):
    return pltpu.roll(block, LANES // 2, 1)


def qkv_kernel(
    tokens_hbm, gain_hbm, weight_hbm, mlp_gain_hbm, out, kept, tokens, gain, weight, sems
):
    loads = [
        pltpu.make_async_copy(tokens_hbm, tokens, sems.at[0]),
        pltpu.make_async_copy(gain_hbm, gain, sems.at[1]),
        pltpu.make_async_copy(weight_hbm, weight, sems.at[2]),
        pltpu.make_async_copy(mlp_gain_hbm, kept.at[1], sems.at[3]),
    ]
    for load in loads:
        load.start()
    t = lax.axis_index("tp")
    loads[0].wait()
    loads[1].wait()
    x = tokens[...].astype(f32)
    row = jnp.sum(jnp.where(row_ids(x.shape) == t, x, 0.0), axis=0, keepdims=True)
    kept[0] = jnp.concatenate([row[:, k * LANES : (k + 1) * LANES] for k in range(8)], axis=0)
    scale = lax.rsqrt(jnp.mean(x * x, axis=-1, keepdims=True) + 1e-05)
    normed = (x * scale * gain[...]).astype(bf16)
    loads[2].wait()
    part = lax.dot_general(normed, weight[...], NT, preferred_element_type=f32)
    part = part.astype(bf16).astype(f32)
    first = part[:, :LANES]
    last = part[:, LANES:]
    turned = half_swap(first)
    lanes = lane_ids(first.shape)
    low = lanes < 64
    blocks = (
        jnp.where(low, first, turned),
        jnp.where(low, turned, first),
        jnp.concatenate([last, last], axis=1),
    )
    placed = []
    for j, block in enumerate(blocks):
        sub = lax.rem(3 * t + j, 2)
        placed.append(jnp.where(lanes // 64 == sub, block, 0.0))
    for head in range(8):
        slot = jnp.zeros(first.shape, f32)
        for j in range(3):
            mine = lax.rem(3 * t + j, 16) // 2 == head
            slot = slot + jnp.where(mine, placed[j], 0.0)
        out[head] = slot.astype(bf16)
        out[head + 8] = slot.astype(bf16)
    loads[3].wait()


def load_kernel(
    lengths_hbm, groups_hbm, span_hbm, pages_hbm, slots_hbm, forget_hbm, rate_hbm,
    pool_hbm, prefix_hbm,
    columns, marks, rates, pool, prefix,
    lengths, groups, span, pages, slots, forget, rate, small_sems, sems,
):
    small = [
        pltpu.make_async_copy(src, dst, small_sems.at[i])
        for i, (src, dst) in enumerate((
            (lengths_hbm, lengths), (groups_hbm, groups), (span_hbm, span), (pages_hbm, pages),
            (slots_hbm, slots), (forget_hbm, forget), (rate_hbm, rate),
        ))
    ]
    big = [
        pltpu.make_async_copy(pool_hbm, pool, sems.at[0]),
        pltpu.make_async_copy(prefix_hbm, prefix, sems.at[1]),
    ]
    for load in small + big:
        load.start()
    t = lax.axis_index("tp")
    half = t // 8
    head = lax.rem(t, 8)
    rows = columns.shape[1]
    for load in small:
        load.wait()
    columns[0] = column(lambda r: lengths[r], rows)
    columns[1] = column(lambda r: groups[r], rows)
    columns[2] = column(lambda r: pages[half, r], rows)
    columns[3] = column(lambda r: span[r], rows)
    mark_row = row_ids(marks.shape)
    marks[...] = jnp.where(mark_row == 0, slots[0, 0], slots[0, 1])
    rates[...] = jnp.where(mark_row == 0, forget[head], rate[head])
    for load in big:
        load.wait()


def pick(recv, kind, head):
    one = (16 * kind + 2 * head) // 3
    two = (16 * kind + 2 * head + 1) // 3
    a = recv[one].astype(f32)
    b = recv[two].astype(f32)
    return jnp.where(one == two, a, a + b)


def attend_kernel(recv, columns, pool, prefix, away_out, here_out):
    t = lax.axis_index("tp")
    half = t // 8
    head = lax.rem(t, 8)
    query = pick(recv, 0, head)
    key = pick(recv, 1, head)
    value = pick(recv, 2, head)
    rows = query.shape[0]
    lanes = lane_ids((rows, LANES))
    low = lanes < 64
    length = columns[0]
    group = columns[1]
    page = columns[2]
    score_scale = LANES ** (-0.5)
    page_count = pool.shape[0]
    query_b = query.astype(bf16)
    pool_keys = pool[:, :, :LANES].reshape(page_count * LANES, LANES)
    pool_scores = lax.dot_general(query_b, pool_keys, NT, preferred_element_type=f32)
    pre_rows = prefix.shape[0] * prefix.shape[1]
    pre_keys = prefix[:, :, :LANES].reshape(pre_rows, LANES)
    pre_scores = lax.dot_general(query_b, pre_keys, NT, preferred_element_type=f32)
    tiles = []
    in_reach = lanes + half * LANES < length
    for p in range(page_count):
        live = (page == p) & in_reach
        tile = pool_scores[:, p * LANES : (p + 1) * LANES] * score_scale
        tiles.append(jnp.where(live, tile, -jnp.inf))
    for p in range(pre_rows // LANES):
        live = group == lanes // 64 + 2 * p
        tile = pre_scores[:, p * LANES : (p + 1) * LANES] * score_scale
        tiles.append(jnp.where(live, tile, -jnp.inf))
    own = jnp.sum(query * key, axis=-1, keepdims=True) * score_scale
    own = jnp.where(half == 0, own, -jnp.inf)
    peak = tiles[0]
    for tile in tiles[1:]:
        peak = jnp.maximum(peak, tile)
    top = jnp.maximum(jnp.max(peak, axis=-1, keepdims=True), own)
    weights = [jnp.exp(tile - top) for tile in tiles]
    own_weight = jnp.exp(own - top)
    total = weights[0]
    for tile in weights[1:]:
        total = total + tile
    denom = jnp.sum(total, axis=-1, keepdims=True) + own_weight

    def both(parts):
        full = jnp.concatenate(parts, axis=1)
        upper = full.astype(bf16)
        lower = (full - upper.astype(f32)).astype(bf16)
        return jnp.concatenate([upper, lower], axis=0)

    pool_values = pool[:, :, LANES:].reshape(page_count * LANES, LANES)
    pre_values = prefix[:, :, LANES:].reshape(pre_rows, LANES)
    summed = jnp.dot(both(weights[:page_count]), pool_values, preferred_element_type=f32)
    summed = summed + jnp.dot(
        both(weights[page_count:]), pre_values, preferred_element_type=f32
    )
    summed = summed[:rows] + summed[rows:] + own_weight * value
    attended = summed / denom
    lse = top + jnp.log(denom)
    swapped = half_swap(attended)
    here_out[...] = jnp.where(low, jnp.where(half == 0, attended, swapped), lse)
    away_out[...] = jnp.where(low, jnp.where(half == 0, swapped, attended), lse)


def memory_kernel(
    slots_hbm, dests_hbm, pages_hbm, memory_hbm, weight_hbm, gate_hbm, up_hbm, down_hbm,
    recv, columns, rates, pool, here,
    memory_out, recalled_out, send_out, pool_out, weight, gate, up, down,
    slots, dests, pages, memory, masked, small_sems, sems, out_sem,
):
    del here
    small = [
        pltpu.make_async_copy(slots_hbm, slots, small_sems.at[0]),
        pltpu.make_async_copy(dests_hbm, dests, small_sems.at[1]),
        pltpu.make_async_copy(pages_hbm, pages, small_sems.at[2]),
    ]
    big = [
        pltpu.make_async_copy(src, dst, sems.at[i])
        for i, (src, dst) in enumerate((
            (memory_hbm, memory), (weight_hbm, weight), (gate_hbm, gate), (up_hbm, up),
            (down_hbm, down),
        ))
    ]
    pool_copy = pltpu.make_async_copy(pool, pool_out, out_sem)
    for load in small + big + [pool_copy]:
        load.start()
    t = lax.axis_index("tp")
    half = t // 8
    head = lax.rem(t, 8)
    query = pick(recv, 0, head)
    key = pick(recv, 1, head)
    value = pick(recv, 2, head)
    rows = query.shape[0]
    shape = query.shape
    lanes = lane_ids(shape)
    row = row_ids(shape)
    low = lanes < 64
    query_unit = query * lax.rsqrt(jnp.sum(query * query, axis=-1, keepdims=True) + 1e-06)
    key_unit = key * lax.rsqrt(jnp.sum(key * key, axis=-1, keepdims=True) + 1e-06)
    mem_rows = memory.shape[1]
    big[0].wait()
    flat_memory = memory[...].reshape(rows * mem_rows, LANES)
    seen = lax.dot_general(
        jnp.concatenate([query_unit, key_unit], axis=0), flat_memory, NT,
        preferred_element_type=f32, precision=highest,
    )
    recalled = jnp.zeros(shape, f32)
    value_half = jnp.where(half == 0, value, half_swap(value))
    value_both = jnp.where(low, value_half, half_swap(value_half))
    closing = columns[3] == 1
    keep = rates[0:1]
    step = rates[1:2]
    for c in range(rows // 2):
        mine = row == 2 * c + lanes // 64
        cut = slice(c * LANES, (c + 1) * LANES)
        recalled = recalled + jnp.where(mine, seen[:rows, cut], 0.0)
        misfit = (value_both - seen[rows:, cut]) * step
        masked[:, cut] = jnp.where(mine & closing, misfit, 0.0)
    recalled_out[...] = recalled + half_swap(recalled)
    change = lax.dot_general(
        masked[...], key_unit, (((0,), (0,)), ((), ())),
        preferred_element_type=f32, precision=highest,
    )
    decay = jnp.where(closing, keep, 1.0)
    for r in range(rows):
        memory_out[r] = decay[r : r + 1] * memory[r] + change[r * mem_rows : (r + 1) * mem_rows]
    for load in small:
        load.wait()
    for m in range(2):
        slot = slots[0, m]
        send_out[m * LANES : (m + 1) * LANES, :] = pool[pages[half, slot]]
        send_out[2 * LANES : 2 * LANES + 64, m * LANES : (m + 1) * LANES] = memory_out[
            slot
        ].astype(bf16)
    code = jnp.where(row_ids((8, 2 * LANES)) == 0, dests[0, 0], dests[0, 1])
    send_out[2 * LANES + 64 :, :] = code.astype(f32).astype(bf16)
    for load in big[1:] + [pool_copy]:
        load.wait()


def spread(rows, wide):
    for k in range(8):
        rows[:, k, :] = wide[:, k * LANES : (k + 1) * LANES]


def project_kernel(here, away, recalled, weight, out, rows):
    mine = here[...]
    other = away[...]
    lse = mine[:, 64:65]
    lse_other = other[:, 64:65]
    share = 1.0 / (1.0 + jnp.exp(lse_other - lse))
    share_other = 1.0 / (1.0 + jnp.exp(lse - lse_other))
    mixed = share * mine + share_other * other + recalled[...]
    mixed = mixed.astype(bf16)[:, :64]
    spread(rows, jnp.dot(mixed, weight[...], preferred_element_type=f32))
    out[...] = rows[...].astype(bf16)


def hidden_kernel(recv, kept, hidden_out, normed_out):
    hidden = kept[0]
    for s in range(recv.shape[0]):
        hidden = hidden + recv[s].astype(f32)
    hidden_out[...] = hidden
    square = jnp.sum(jnp.sum(hidden * hidden, axis=1, keepdims=True), axis=0, keepdims=True)
    scale = lax.rsqrt(square / (8 * LANES) + 1e-05)
    normed = (hidden * scale * kept[1]).astype(bf16)
    for s in range(normed_out.shape[0]):
        normed_out[s] = normed


def mlp_kernel(recv, gate_weight, up_weight, down_weight, out, rows):
    rows[...] = recv[...].astype(f32)
    x = jnp.concatenate([rows[:, k, :] for k in range(8)], axis=1).astype(bf16)
    gate = lax.dot_general(x, gate_weight[...], NT, preferred_element_type=f32)
    up = lax.dot_general(x, up_weight[...], NT, preferred_element_type=f32)
    active = (gate * (1.0 / (1.0 + jnp.exp(-gate))) * up).astype(bf16)
    spread(rows, jnp.dot(active, down_weight[...], preferred_element_type=f32))
    out[...] = rows[...].astype(bf16)


def row_kernel(recv, hidden, out):
    total = hidden[...]
    for s in range(recv.shape[0]):
        total = total + recv[s].astype(f32)
    row = total.astype(bf16)
    for s in range(16):
        out[s] = row


def leave_kernel(marks, recv, out):
    leaving = []
    for m in range(2):
        mark = marks[m : m + 1]
        row = jnp.zeros(recv.shape[1:], f32)
        for s in range(recv.shape[0]):
            row = jnp.where(mark == s, recv[s].astype(f32), row)
        leaving.append(row)
    both = jnp.concatenate(leaving, axis=0).astype(bf16)
    for s in range(out.shape[0]):
        out[s] = both


def place_kernel(
    pages_hbm, slots_hbm, pool, memory, gathered, pool_out, memory_out, codes_out,
    pages, slots, codes, page, raw, wide, small_sems, page_sem, raw_sem, wide_sem,
):
    small = [
        pltpu.make_async_copy(pages_hbm, pages, small_sems.at[0]),
        pltpu.make_async_copy(slots_hbm, slots, small_sems.at[1]),
        pltpu.make_async_copy(
            gathered.at[:, pl.ds(2 * LANES + 64, 8), pl.ds(0, LANES)], codes, small_sems.at[2]
        ),
    ]
    for load in small:
        load.start()
    half = lax.axis_index("tp") // 8
    me = lax.axis_index("rep").astype(f32)
    for load in small:
        load.wait()
    all_codes = codes[...].astype(f32)
    codes_out[...] = all_codes
    row = row_ids((codes.shape[0], LANES))
    moved = []
    for m in range(2):
        source = jnp.max(jnp.where(codes_out[:, m, :] == me, row, 0))
        page_in = pltpu.make_async_copy(
            gathered.at[source, pl.ds(m * LANES, LANES), :], page.at[m], page_sem.at[m]
        )
        raw_in = pltpu.make_async_copy(
            gathered.at[source, pl.ds(2 * LANES, 64), pl.ds(m * LANES, LANES)],
            raw.at[m],
            raw_sem.at[m],
        )
        page_in.start()
        raw_in.start()
        moved.append((page_in, raw_in))
    stores = []
    for m in range(2):
        moved[m][0].wait()
        place = pool_out.at[pages[half, slots[0, m]]]
        stores.append(pltpu.make_async_copy(page.at[m], place, page_sem.at[2 + m]))
        stores[-1].start()
    for m in range(2):
        moved[m][1].wait()
        wide[m] = raw[m].astype(f32)
        place = memory_out.at[slots[0, m]]
        stores.append(pltpu.make_async_copy(wide.at[m], place, wide_sem.at[m]))
        stores[-1].start()
    for store in stores:
        store.wait()


def rows_kernel(marks, rows_all, recv, codes, rows_out, rows):
    me = lax.axis_index("rep").astype(f32)
    arriving = []
    for m in range(2):
        row = jnp.zeros(rows_all.shape[1:], f32)
        for s in range(recv.shape[0]):
            part = recv[s, 8 * m : 8 * m + 8, :].astype(f32)
            row = jnp.where(codes[s, m : m + 1, :] == me, part, row)
        arriving.append(row)
    for s in range(rows_all.shape[0]):
        row = rows_all[s].astype(f32)
        for m in range(2):
            row = jnp.where(marks[m : m + 1] == s, arriving[m], row)
        rows[s] = row
    for k in range(8):
        rows_out[:, k * LANES : (k + 1) * LANES] = rows[:, k, :].astype(bf16)


def body(
    tokens,
    lengths,
    prompt_group,
    span_close,
    out_slot,
    move_dest,
    page_table,
    cache_pool,
    prefix_cache,
    memory,
    norm_attn,
    norm_mlp,
    qkv_weight,
    out_weight,
    gate_weight,
    up_weight,
    down_weight,
    forget,
    write_rate,
):
    shape = jax.ShapeDtypeStruct
    rows = tokens.shape[0]
    n_tp = lax.axis_size("tp")
    n_rep = lax.axis_size("rep")
    pages = page_table.transpose(2, 1, 0)[0]
    pool = cache_pool[:, 0]
    prefix = prefix_cache[:, 0]
    mem = memory[:, 0]
    send_shape = shape((2 * LANES + 72, 2 * LANES), bf16)

    qkv_slots, kept = call(
        qkv_kernel,
        (shape((n_tp, rows, LANES), bf16), shape((2, 8, LANES), f32)),
        [HBM] * 4,
        scratch=[
            pltpu.VMEM(tokens.shape, bf16),
            pltpu.VMEM((1, tokens.shape[1]), f32),
            pltpu.VMEM(qkv_weight.shape[::-1], bf16),
            pltpu.SemaphoreType.DMA((4,)),
        ],
    )(*in_hbm(tokens, norm_attn.reshape(1, -1), qkv_weight.T, norm_mlp.reshape(8, LANES)))
    qkv_recv = lax.all_to_all(qkv_slots, "tp", 0, 0)

    gate = gate_weight.T
    up = up_weight.T
    columns, marks, rates, pool_near, prefix_near = call(
        load_kernel,
        (
            shape((4, rows, LANES), jnp.int32),
            shape((8, LANES), jnp.int32),
            shape((8, LANES), f32),
            shape(pool.shape, bf16),
            shape(prefix.shape, bf16),
        ),
        [HBM] * 9,
        scratch=[
            pltpu.SMEM((rows,), jnp.int32),
            pltpu.SMEM((rows,), jnp.int32),
            pltpu.SMEM((rows,), jnp.int32),
            pltpu.SMEM(pages.shape, jnp.int32),
            pltpu.SMEM(out_slot.shape, jnp.int32),
            pltpu.SMEM(forget.shape, f32),
            pltpu.SMEM(write_rate.shape, f32),
            pltpu.SemaphoreType.DMA((7,)),
            pltpu.SemaphoreType.DMA((2,)),
        ],
    )(
        *in_hbm(lengths, prompt_group, span_close, pages, out_slot, forget, write_rate),
        *in_hbm(pool, prefix),
    )

    away, here = call(
        attend_kernel, (shape((rows, LANES), f32), shape((rows, LANES), f32)), [VMEM] * 4
    )(qkv_recv, columns, pool_near, prefix_near)
    away_recv = lax.ppermute(away, "tp", [(i, (i + n_tp // 2) % n_tp) for i in range(n_tp)])
    mem_after, recalled, send, pool_base, out_near, gate_near, up_near, down_near = call(
        memory_kernel,
        (
            shape(mem.shape, f32),
            shape((rows, LANES), f32),
            send_shape,
            shape(pool.shape, bf16),
            shape(out_weight.shape, bf16),
            shape(gate.shape, bf16),
            shape(up.shape, bf16),
            shape(down_weight.shape, bf16),
        ),
        [HBM] * 8 + [VMEM] * 4 + [HBM],
        out_specs=(VMEM,) * 3 + (HBM,) + (VMEM,) * 4,
        scratch=[
            pltpu.SMEM(out_slot.shape, jnp.int32),
            pltpu.SMEM(move_dest.shape, jnp.int32),
            pltpu.SMEM(pages.shape, jnp.int32),
            pltpu.VMEM(mem.shape, f32),
            pltpu.VMEM((rows, rows * 64), f32),
            pltpu.SemaphoreType.DMA((3,)),
            pltpu.SemaphoreType.DMA((5,)),
            pltpu.SemaphoreType.DMA,
        ],
    )(
        *in_hbm(out_slot, move_dest, pages, mem, out_weight, gate, up, down_weight),
        qkv_recv, columns, rates, pool_near, here,
    )
    gathered = lax.all_gather(send, "rep", axis=0)

    row_scratch = pltpu.VMEM((rows, 8, LANES), f32)
    terms = call(
        project_kernel, shape((n_tp, 8, LANES), bf16), [VMEM] * 4, scratch=[row_scratch]
    )(here, away_recv, recalled, out_near)
    terms_recv = lax.all_to_all(terms, "tp", 0, 0)

    hidden, normed_slots = call(
        hidden_kernel,
        (shape((8, LANES), f32), shape((n_tp, 8, LANES), bf16)),
        [VMEM] * 2,
    )(terms_recv, kept)
    normed_recv = lax.all_to_all(normed_slots, "tp", 0, 0)

    down_slots = call(
        mlp_kernel, shape((n_tp, 8, LANES), bf16), [VMEM] * 4, scratch=[row_scratch]
    )(normed_recv, gate_near, up_near, down_near)
    down_recv = lax.all_to_all(down_slots, "tp", 0, 0)

    row_slots = call(row_kernel, shape((n_tp, 8, LANES), bf16), [VMEM] * 2)(down_recv, hidden)
    rows_all = lax.all_to_all(row_slots, "tp", 0, 0)

    leaving = call(leave_kernel, shape((n_rep, 16, LANES), bf16), [VMEM] * 2)(marks, rows_all)
    arrived = lax.all_to_all(leaving, "rep", 0, 0)

    pool_out, mem_out, codes = call(
        place_kernel,
        (shape(pool.shape, bf16), shape(mem.shape, f32), shape((n_rep, 8, LANES), f32)),
        [HBM] * 5,
        out_specs=(HBM, HBM, VMEM),
        scratch=[
            pltpu.SMEM(pages.shape, jnp.int32),
            pltpu.SMEM(out_slot.shape, jnp.int32),
            pltpu.VMEM((n_rep, 8, LANES), bf16),
            pltpu.VMEM((2, LANES, 2 * LANES), bf16),
            pltpu.VMEM((2, 64, LANES), bf16),
            pltpu.VMEM((2, 64, LANES), f32),
            pltpu.SemaphoreType.DMA((3,)),
            pltpu.SemaphoreType.DMA((4,)),
            pltpu.SemaphoreType.DMA((2,)),
            pltpu.SemaphoreType.DMA((2,)),
        ],
        aliases={2: 0, 3: 1},
    )(*in_hbm(pages, out_slot, pool_base, mem_after, gathered))
    rows_out = call(
        rows_kernel, shape(tokens.shape, bf16), [VMEM] * 4, scratch=[row_scratch]
    )(marks, rows_all, arrived, codes)
    return rows_out, mem_out[:, None], pool_out[:, None]


def solution(mesh):
    placed = (
        P("rep", None),
        P("rep"),
        P("rep"),
        P("rep"),
        P("rep", None),
        P("rep", None),
        P("rep", None, None),
        P("rep", "tp", None, None),
        P(None, "tp", None, None),
        P("rep", "tp", None, None),
        P(),
        P(),
        P(None, "tp"),
        P("tp", None),
        P(None, "tp"),
        P(None, "tp"),
        P("tp", None),
        P(),
        P(),
    )
    return jax.shard_map(
        body,
        mesh=mesh,
        in_specs=placed,
        out_specs=(P("rep", None), P("rep", "tp", None, None), P("rep", "tp", None, None)),
        check_vma=False,
    )
```

time: 166 us -> 143 us (0.86)
  blocking collectives: 78.9 us -> 56.2 us
  local copies, waits for them, and re-layouts: 15.5 us -> 0 us
  waiting for transfers between devices: 12.6 us -> 24.5 us
  starting transfers between devices: 31.3 us -> 34.6 us
    unnamed x40 -> x0, local copies, waits for them, and re-layouts: 15.4 us -> none
    all_to_all x1, blocking collectives: 28.4 us -> 14.4 us  [body(): terms_recv = lax.all_to_all(terms, 'tp', 0, 0)]
    all_to_all x1, starting transfers between devices: 3.5 us -> 15.1 us  [body(): arrived = lax.all_to_all(leaving, 'rep', 0, 0)]
    all_to_all x1, waiting for transfers between devices: 0.01 us -> 10.2 us  [body(): qkv_recv = lax.all_to_all(qkv_slots, 'tp', 0, 0)]
    all_to_all x1, blocking collectives: 22.6 us -> 14 us  [body(): normed_recv = lax.all_to_all(normed_slots, 'tp', 0, 0)]
    ppermute x1, starting transfers between devices: 12 us -> 3.69 us  [body(): lax.ppermute(away, 'tp', [(i, (i + n_tp // 2) % n_tp) for i in range(n_tp)])]
    ppermute x1, waiting for transfers between devices: 3.56 us -> 9.41 us  [body(): lax.ppermute(away, 'tp', [(i, (i + n_tp // 2) % n_tp) for i in range(n_tp)])]
    all_to_all x1, waiting for transfers between devices: 9.02 us -> 4.88 us  [body(): arrived = lax.all_to_all(leaving, 'rep', 0, 0)]
  transfers between devices with their start and end apart: 4 -> 4, of which waited for: 2 -> 3; matrix products, arithmetic and copies ran while one was open for 2% -> 0% of each run, Pallas kernels for 1% -> 4%
where the time goes in v2:
time: 143 us; the launch traced here: 142 us
  blocking collectives  56.2 us (39%)
  starting transfers between devices  34.6 us (24%)
  waiting for transfers between devices  24.5 us (17%)
  between operations  14.1 us (10%)
  Pallas kernels  12.6 us (9%)
    all_to_all x1, starting transfers between devices, body(): qkv_recv = lax.all_to_all(qkv_slots, 'tp', 0, 0)  15.8 us
    all_to_all x1, starting transfers between devices, body(): arrived = lax.all_to_all(leaving, 'rep', 0, 0)  15.1 us
    all_to_all x1, blocking collectives, body(): terms_recv = lax.all_to_all(terms, 'tp', 0, 0)  14.4 us
    all_to_all x1, blocking collectives, body(): down_recv = lax.all_to_all(down_slots, 'tp', 0, 0)  14 us
    all_to_all x1, blocking collectives, body(): normed_recv = lax.all_to_all(normed_slots, 'tp', 0, 0)  14 us
    all_to_all x1, blocking collectives, body(): rows_all = lax.all_to_all(row_slots, 'tp', 0, 0)  13.8 us
    all_to_all x1, waiting for transfers between devices, body(): qkv_recv = lax.all_to_all(qkv_slots, 'tp', 0, 0)  10.2 us
    ppermute x1, waiting for transfers between devices, body(): lax.ppermute(away, 'tp', [(i, (i + n_tp // 2) % n_tp) for i in range(n_tp)])  9.41 us
  transfers between devices with their start and end apart: 4, of which 3 were waited for; matrix products, arithmetic and copies ran while one was open for 0% of the time, Pallas kernels for 4%

profile of v2, /device:TPU:1, one launch (start us, length us, event | category | flops | bytes accessed | tf_op | source)
XLA Modules:
  0.0 142.0 jit_solution(10585518726074633819)
XLA Ops:
  7.2 2.0 %shard_map.203 = (bf16[16,16,128]{2,1,0:T(8,128)(2,1)}, f32[2,8,128]{2,1,0:T(8,128)S(1)}) custom-call(bf16[16,1024]{1,0:T(8,128)(2,1)} %tokens_hbm.1, f32[1,1024]{1,0:T(1,128)} %bitcast.30, bf16[192,1024]{1,0:T(8,128)(2,1)} %bitcast.23, f32[8,128]{1,0:T(8,128)} %bitcast.31), custom_call_target="tpu_custom_call" | custom-call | tf_op jit(solution)/shard_map/pallas_call | solution.py:446
  9.2 15.8 %all-to-all-start = ((bf16[16,16,128]{2,1,0:T(8,128)(2,1)}), bf16[16,16,128]{2,1,0:T(8,128)(2,1)S(1)}, u32[]{:S(2)}, u32[]{:S(2)}) async-start(bf16[16,16,128]{2,1,0:T(8,128)(2,1)} %get-tuple-element.26), calls=%async_computation | async-start | bytes 131072 | tf_op jit(solution)/shard_map/all_to_all | solution.py:457
  24.9 0.0 all-gather.3.cloned.1.call-start
  25.0 1.4 shard_map.202
  26.4 10.2 %all-to-all-done.recv = bf16[16,16,128]{2,1,0:T(8,128)(2,1)S(1)} async-done(((bf16[16,16,128]{2,1,0:T(8,128)(2,1)}), bf16[16,16,128]{2,1,0:T(8,128)(2,1)S(1)}, u32[]{:S(2)}, u32[]{:S(2)}) %all-to-all-start) | async-done | bytes 65568 | tf_op jit(solution)/shard_map/all_to_all | solution.py:457
  36.5 0.6 shard_map.204
  37.2 3.5 %shard_map.205 = (f32[16,64,128]{2,1,0:T(8,128)}, f32[16,128]{1,0:T(8,128)S(1)}, bf16[328,256]{1,0:T(8,128)(2,1)}, bf16[16,128,256]{2,1,0:T(8,128)(2,1)}, bf16[6...) custom-call(s32[1,2]{1,0:T(1,128)} %slots_hbm.5, ...), custom_call_target="tpu_custom_call" | custom-call | tf_op jit(solution)/shard_map/pallas_call | solution.py:491
  40.7 0.0 all-gather.3.cloned.1.call-update
  40.7 3.7 %collective-permute-start = (f32[16,128]{1,0:T(8,128)S(1)}, f32[16,128]{1,0:T(8,128)S(1)}, u32[]{:S(2)}, u32[]{:S(2)}) collective-permute-start(f32[16,128]{1,0:T(8,128)S(1)} %get-tuple-element.31), channel_id=1, source_target_pairs={{0,8},{1,9},{2,10},{3,11},{4,12},{5,13},{6,14},{7,15},{8,0},{9,1},... | collective-permute-start | bytes 24584 | tf_op jit(solution)/shard_map/ppermute | solution.py:490
  44.4 9.4 %collective-permute-done.away = f32[16,128]{1,0:T(8,128)S(1)} collective-permute-done((f32[16,128]{1,0:T(8,128)S(1)}, f32[16,128]{1,0:T(8,128)S(1)}, u32[]{:S(2)}, u32[]{:S(2)}) %collective-permute-start) | collective-permute-done | bytes 8224 | tf_op jit(solution)/shard_map/ppermute | solution.py:490
  53.8 0.2 shard_map.206
  54.1 14.4 %all_to_all.30.recv = bf16[16,8,128]{2,1,0:T(8,128)(2,1)S(1)} all-to-all(bf16[16,8,128]{2,1,0:T(8,128)(2,1)S(1)} %shard_map.206), channel_id=1, replica_groups=mesh['rep'=32,'tp'=16] {'tp'}, dimensions={0} | all-to-all | bytes 65536 | tf_op jit(solution)/shard_map/all_to_all | solution.py:525
  68.5 0.1 shard_map.207
  68.6 14.0 %all_to_all.31.recv = bf16[16,8,128]{2,1,0:T(8,128)(2,1)S(1)} all-to-all(bf16[16,8,128]{2,1,0:T(8,128)(2,1)S(1)} %get-tuple-element.36), channel_id=1, replica_groups=mesh['rep'=32,'tp'=16] {'tp'}, dimensions={0} | all-to-all | bytes 65536 | tf_op jit(solution)/shard_map/all_to_all | solution.py:532
  82.6 0.5 shard_map.208
  83.1 14.0 %all_to_all.32.recv = bf16[16,8,128]{2,1,0:T(8,128)(2,1)S(1)} all-to-all(bf16[16,8,128]{2,1,0:T(8,128)(2,1)S(1)} %shard_map.208), channel_id=1, replica_groups=mesh['rep'=32,'tp'=16] {'tp'}, dimensions={0} | all-to-all | bytes 65536 | tf_op jit(solution)/shard_map/all_to_all | solution.py:537
  97.1 13.8 %all_to_all.33.recv.rows_all = bf16[16,8,128]{2,1,0:T(8,128)(2,1)S(1)} all-to-all(bf16[16,8,128]{2,1,0:T(8,128)(2,1)S(1)} %shard_map.209), channel_id=1, replica_groups=mesh['rep'=32,'tp'=16] {'tp'}, dimensions={0} | all-to-all | bytes 65536 | tf_op jit(solution)/shard_map/all_to_all | solution.py:540
  110.9 0.7 shard_map.210
  111.6 15.1 %all-to-all-start.5 = ((bf16[32,16,128]{2,1,0:T(8,128)(2,1)}), bf16[32,16,128]{2,1,0:T(8,128)(2,1)S(1)}, u32[]{:S(2)}, u32[]{:S(2)}) async-start(bf16[32,16,128]{2,1,0:T(8,128)(2,1)} %shard_map.210), calls=%async_computation.5 | async-start | bytes 262144 | tf_op jit(solution)/shard_map/all_to_all | solution.py:543
  126.8 0.0 all-gather.3.cloned.1.call-done
  126.8 2.7 %shard_map.211 = (bf16[16,128,256]{2,1,0:T(8,128)(2,1)}, f32[16,64,128]{2,1,0:T(8,128)}, f32[32,8,128]{2,1,0:T(8,128)S(1)}) custom-call(s32[2,16]{1,0:T(2,128)} %bitcast.29, s32[1,2]{1,0:T(1,128)} %slots_hbm.5, bf16[16,128,256]{2,1,0:T(8,128)(2,1)} %get-tuple-element.41.pool, ...), custom_call_target="tpu_custom_call", output_to_operand_aliasing={{0}: (2, {}), {1}: (3, {})} | custom-call | tf_op jit(solution)/shard_map/pallas_call | solution.py:545
  129.5 4.9 %all-to-all-done.5.recv = bf16[32,16,128]{2,1,0:T(8,128)(2,1)S(1)} async-done(((bf16[32,16,128]{2,1,0:T(8,128)(2,1)}), bf16[32,16,128]{2,1,0:T(8,128)(2,1)S(1)}, u32[]{:S(2)}, u32[]{:S(2)}) %all-to-all-start.5) | async-done | bytes 131104 | tf_op jit(solution)/shard_map/all_to_all | solution.py:543
  134.4 0.8 shard_map.212
  (1 shorter events, 0.0 us)
Async XLA Ops:
  9.2 27.3 %all-to-all-start = ((bf16[16,16,128]{2,1,0:T(8,128)(2,1)}), bf16[16,16,128]{2,1,0:T(8,128)(2,1)S(1)}, u32[]{:S(2)}, u32[]{:S(2)}) async-start(bf16[16,16,128]{2,1,0:T(8,128)(2,1)} %get-tuple-element.26), calls=%async_computation | async-start | bytes 131072 | tf_op jit(solution)/shard_map/all_to_all | solution.py:457
  24.9 101.8 %all-gather.3.cloned.1.call-start = ((), (), s32[]{:S(2)}) async-start(), calls=%async_computation.6 | async-start | bytes 5541888 | tf_op jit(solution)/shard_map/all_gather | solution.py:519
  40.7 13.1 %collective-permute-start = (f32[16,128]{1,0:T(8,128)S(1)}, f32[16,128]{1,0:T(8,128)S(1)}, u32[]{:S(2)}, u32[]{:S(2)}) collective-permute-start(f32[16,128]{1,0:T(8,128)S(1)} %get-tuple-element.31), channel_id=1, source_target_pairs={{0,8},{1,9},{2,10},{3,11},{4,12},{5,13},{6,14},{7,15},{8,0},{9,1},... | collective-permute-start | bytes 24584 | tf_op jit(solution)/shard_map/ppermute | solution.py:490
  111.6 22.8 %all-to-all-start.5 = ((bf16[32,16,128]{2,1,0:T(8,128)(2,1)}), bf16[32,16,128]{2,1,0:T(8,128)(2,1)S(1)}, u32[]{:S(2)}, u32[]{:S(2)}) async-start(bf16[32,16,128]{2,1,0:T(8,128)(2,1)} %shard_map.210), calls=%async_computation.5 | async-start | bytes 262144 | tf_op jit(solution)/shard_map/all_to_all | solution.py:543
Sparse Core Ops, SparseCore 0:
  40.8 57.0 all-gather.2

commit v3 on v2

--- a/solution.py
+++ b/solution.py
@@ -100,8 +100,8 @@
 
 def load_kernel(
     lengths_hbm, groups_hbm, span_hbm, pages_hbm, slots_hbm, forget_hbm, rate_hbm,
-    pool_hbm, prefix_hbm,
-    columns, marks, rates, pool, prefix,
+    pool_hbm, prefix_hbm, memory_hbm, weight_hbm, gate_hbm, up_hbm, down_hbm,
+    columns, marks, rates, pool, prefix, memory, weight, gate, up, down,
     lengths, groups, span, pages, slots, forget, rate, small_sems, sems,
 ):
     small = [
@@ -112,8 +112,11 @@
         ))
     ]
     big = [
-        pltpu.make_async_copy(pool_hbm, pool, sems.at[0]),
-        pltpu.make_async_copy(prefix_hbm, prefix, sems.at[1]),
+        pltpu.make_async_copy(src, dst, sems.at[i])
+        for i, (src, dst) in enumerate((
+            (pool_hbm, pool), (prefix_hbm, prefix), (memory_hbm, memory), (weight_hbm, weight),
+            (gate_hbm, gate), (up_hbm, up), (down_hbm, down),
+        ))
     ]
     for load in small + big:
         load.start()
@@ -142,7 +145,18 @@
     return jnp.where(one == two, a, a + b)
 
 
-def attend_kernel(recv, columns, pool, prefix, away_out, here_out):
+def attend_kernel(
+    slots_hbm, dests_hbm, pages_hbm, recv, columns, rates, pool, prefix, memory,
+    away_out, here_out, send_out,
+    slots, dests, pages, small_sems,
+):
+    small = [
+        pltpu.make_async_copy(slots_hbm, slots, small_sems.at[0]),
+        pltpu.make_async_copy(dests_hbm, dests, small_sems.at[1]),
+        pltpu.make_async_copy(pages_hbm, pages, small_sems.at[2]),
+    ]
+    for load in small:
+        load.start()
     t = lax.axis_index("tp")
     half = t // 8
     head = lax.rem(t, 8)
@@ -205,29 +219,36 @@
     here_out[...] = jnp.where(low, jnp.where(half == 0, attended, swapped), lse)
     away_out[...] = jnp.where(low, jnp.where(half == 0, swapped, attended), lse)
 
+    key_unit = key * lax.rsqrt(jnp.sum(key * key, axis=-1, keepdims=True) + 1e-06)
+    value_half = jnp.where(half == 0, value, half_swap(value))
+    closing = columns[3]
+    row = row_ids(lanes.shape)
+    mem_shape = memory.shape[1:]
+    diagonal = row_ids(mem_shape) == lane_ids(mem_shape)
+    for load in small:
+        load.wait()
+    for m in range(2):
+        slot = slots[0, m]
+        mine = row == slot
+        key_row = jnp.sum(jnp.where(mine, key_unit, 0.0), axis=0, keepdims=True)
+        value_row = jnp.sum(jnp.where(mine, value_half, 0.0), axis=0, keepdims=True)
+        closes = jnp.max(jnp.where(mine, closing, 0), axis=0, keepdims=True) == 1
+        block = memory[slot]
+        seen = jnp.sum(block * key_row, axis=1, keepdims=True)
+        target = jnp.sum(jnp.where(diagonal, value_row, 0.0), axis=1, keepdims=True)
+        written = rates[0:1] * block + rates[1:2] * (target - seen) * key_row
+        written = jnp.where(closes, written, block)
+        send_out[m * LANES : (m + 1) * LANES, :] = pool[pages[half, slot]]
+        send_out[2 * LANES : 2 * LANES + 64, m * LANES : (m + 1) * LANES] = written.astype(bf16)
+    code = jnp.where(row_ids((8, 2 * LANES)) == 0, dests[0, 0], dests[0, 1])
+    send_out[2 * LANES + 64 :, :] = code.astype(f32).astype(bf16)
+
 
 def memory_kernel(
-    slots_hbm, dests_hbm, pages_hbm, memory_hbm, weight_hbm, gate_hbm, up_hbm, down_hbm,
-    recv, columns, rates, pool, here,
-    memory_out, recalled_out, send_out, pool_out, weight, gate, up, down,
-    slots, dests, pages, memory, masked, small_sems, sems, out_sem,
+    recv, columns, rates, pool, memory, memory_out, recalled_out, pool_out, masked, out_sem
 ):
-    del here
-    small = [
-        pltpu.make_async_copy(slots_hbm, slots, small_sems.at[0]),
-        pltpu.make_async_copy(dests_hbm, dests, small_sems.at[1]),
-        pltpu.make_async_copy(pages_hbm, pages, small_sems.at[2]),
-    ]
-    big = [
-        pltpu.make_async_copy(src, dst, sems.at[i])
-        for i, (src, dst) in enumerate((
-            (memory_hbm, memory), (weight_hbm, weight), (gate_hbm, gate), (up_hbm, up),
-            (down_hbm, down),
-        ))
-    ]
     pool_copy = pltpu.make_async_copy(pool, pool_out, out_sem)
-    for load in small + big + [pool_copy]:
-        load.start()
+    pool_copy.start()
     t = lax.axis_index("tp")
     half = t // 8
     head = lax.rem(t, 8)
@@ -242,7 +263,6 @@
     query_unit = query * lax.rsqrt(jnp.sum(query * query, axis=-1, keepdims=True) + 1e-06)
     key_unit = key * lax.rsqrt(jnp.sum(key * key, axis=-1, keepdims=True) + 1e-06)
     mem_rows = memory.shape[1]
-    big[0].wait()
     flat_memory = memory[...].reshape(rows * mem_rows, LANES)
     seen = lax.dot_general(
         jnp.concatenate([query_unit, key_unit], axis=0), flat_memory, NT,
@@ -268,18 +288,7 @@
     decay = jnp.where(closing, keep, 1.0)
     for r in range(rows):
         memory_out[r] = decay[r : r + 1] * memory[r] + change[r * mem_rows : (r + 1) * mem_rows]
-    for load in small:
-        load.wait()
-    for m in range(2):
-        slot = slots[0, m]
-        send_out[m * LANES : (m + 1) * LANES, :] = pool[pages[half, slot]]
-        send_out[2 * LANES : 2 * LANES + 64, m * LANES : (m + 1) * LANES] = memory_out[
-            slot
-        ].astype(bf16)
-    code = jnp.where(row_ids((8, 2 * LANES)) == 0, dests[0, 0], dests[0, 1])
-    send_out[2 * LANES + 64 :, :] = code.astype(f32).astype(bf16)
-    for load in big[1:] + [pool_copy]:
-        load.wait()
+    pool_copy.wait()
 
 
 def spread(rows, wide):
@@ -458,7 +467,7 @@
 
     gate = gate_weight.T
     up = up_weight.T
-    columns, marks, rates, pool_near, prefix_near = call(
+    loaded = call(
         load_kernel,
         (
             shape((4, rows, LANES), jnp.int32),
@@ -466,8 +475,13 @@
             shape((8, LANES), f32),
             shape(pool.shape, bf16),
             shape(prefix.shape, bf16),
+            shape(mem.shape, f32),
+            shape(out_weight.shape, bf16),
+            shape(gate.shape, bf16),
+            shape(up.shape, bf16),
+            shape(down_weight.shape, bf16),
         ),
-        [HBM] * 9,
+        [HBM] * 14,
         scratch=[
             pltpu.SMEM((rows,), jnp.int32),
             pltpu.SMEM((rows,), jnp.int32),
@@ -477,46 +491,39 @@
             pltpu.SMEM(forget.shape, f32),
             pltpu.SMEM(write_rate.shape, f32),
             pltpu.SemaphoreType.DMA((7,)),
-            pltpu.SemaphoreType.DMA((2,)),
+            pltpu.SemaphoreType.DMA((7,)),
         ],
     )(
         *in_hbm(lengths, prompt_group, span_close, pages, out_slot, forget, write_rate),
-        *in_hbm(pool, prefix),
-    )
-
-    away, here = call(
-        attend_kernel, (shape((rows, LANES), f32), shape((rows, LANES), f32)), [VMEM] * 4
-    )(qkv_recv, columns, pool_near, prefix_near)
-    away_recv = lax.ppermute(away, "tp", [(i, (i + n_tp // 2) % n_tp) for i in range(n_tp)])
-    mem_after, recalled, send, pool_base, out_near, gate_near, up_near, down_near = call(
-        memory_kernel,
-        (
-            shape(mem.shape, f32),
-            shape((rows, LANES), f32),
-            send_shape,
-            shape(pool.shape, bf16),
-            shape(out_weight.shape, bf16),
-            shape(gate.shape, bf16),
-            shape(up.shape, bf16),
-            shape(down_weight.shape, bf16),
-        ),
-        [HBM] * 8 + [VMEM] * 4 + [HBM],
-        out_specs=(VMEM,) * 3 + (HBM,) + (VMEM,) * 4,
+        *in_hbm(pool, prefix, mem, out_weight, gate, up, down_weight),
+    )
+
+    columns, marks, rates, pool_near, prefix_near, mem_near = loaded[:6]
+    out_near, gate_near, up_near, down_near = loaded[6:]
+
+    away, here, send = call(
+        attend_kernel,
+        (shape((rows, LANES), f32), shape((rows, LANES), f32), send_shape),
+        [HBM] * 3 + [VMEM] * 6,
         scratch=[
             pltpu.SMEM(out_slot.shape, jnp.int32),
             pltpu.SMEM(move_dest.shape, jnp.int32),
             pltpu.SMEM(pages.shape, jnp.int32),
-            pltpu.VMEM(mem.shape, f32),
-            pltpu.VMEM((rows, rows * 64), f32),
             pltpu.SemaphoreType.DMA((3,)),
-            pltpu.SemaphoreType.DMA((5,)),
-            pltpu.SemaphoreType.DMA,
         ],
     )(
-        *in_hbm(out_slot, move_dest, pages, mem, out_weight, gate, up, down_weight),
-        qkv_recv, columns, rates, pool_near, here,
+        *in_hbm(out_slot, move_dest, pages),
+        qkv_recv, columns, rates, pool_near, prefix_near, mem_near,
     )
     gathered = lax.all_gather(send, "rep", axis=0)
+    away_recv = lax.ppermute(away, "tp", [(i, (i + n_tp // 2) % n_tp) for i in range(n_tp)])
+    mem_after, recalled, pool_base = call(
+        memory_kernel,
+        (shape(mem.shape, f32), shape((rows, LANES), f32), shape(pool.shape, bf16)),
+        [VMEM] * 5,
+        out_specs=(VMEM, VMEM, HBM),
+        scratch=[pltpu.VMEM((rows, rows * 64), f32), pltpu.SemaphoreType.DMA],
+    )(qkv_recv, columns, rates, pool_near, mem_near)
 
     row_scratch = pltpu.VMEM((rows, 8, LANES), f32)
     terms = call(

time: 143 us -> 140 us (0.979)
  waiting for transfers between devices: 24.5 us -> 21.8 us
    ppermute x1, waiting for transfers between devices: 9.41 us -> 7.35 us  [body(): lax.ppermute(away, 'tp', [(i, (i + n_tp // 2) % n_tp) for i in range(n_tp)])]
    pallas_call x1, Pallas kernels: 3.53 us -> 2.05 us  [body(): call(memory_kernel, (shape(mem.shape, f32), shape((rows, LANES), f32), sh...]
  transfers between devices with their start and end apart: 4 -> 4, of which waited for: 3 -> 3; matrix products, arithmetic and copies ran while one was open for 0% -> 0% of each run, Pallas kernels for 4% -> 6%
where the time goes in v3:
time: 140 us
  blocking collectives  56.2 us (40%)
  starting transfers between devices  34.6 us (25%)
  waiting for transfers between devices  21.8 us (16%)
  between operations  14.1 us (10%)
  Pallas kernels  12.9 us (9%)
    all_to_all x1, starting transfers between devices, body(): qkv_recv = lax.all_to_all(qkv_slots, 'tp', 0, 0)  15.8 us
    all_to_all x1, starting transfers between devices, body(): arrived = lax.all_to_all(leaving, 'rep', 0, 0)  15.1 us
    all_to_all x1, blocking collectives, body(): terms_recv = lax.all_to_all(terms, 'tp', 0, 0)  14.4 us
    all_to_all x1, blocking collectives, body(): down_recv = lax.all_to_all(down_slots, 'tp', 0, 0)  14 us
    all_to_all x1, blocking collectives, body(): normed_recv = lax.all_to_all(normed_slots, 'tp', 0, 0)  14 us
    all_to_all x1, blocking collectives, body(): rows_all = lax.all_to_all(row_slots, 'tp', 0, 0)  13.8 us
    all_to_all x1, waiting for transfers between devices, body(): qkv_recv = lax.all_to_all(qkv_slots, 'tp', 0, 0)  9.58 us
    ppermute x1, waiting for transfers between devices, body(): lax.ppermute(away, 'tp', [(i, (i + n_tp // 2) % n_tp) for i in range(n_tp)])  7.35 us
  transfers between devices with their start and end apart: 4, of which 3 were waited for; matrix products, arithmetic and copies ran while one was open for 0% of the time, Pallas kernels for 6%

profile of v3, /device:TPU:1, one launch (start us, length us, event | category | flops | bytes accessed | tf_op | source)
XLA Modules:
  0.0 139.7 jit_solution(8652731088046717401)
XLA Ops:
  7.2 2.0 %shard_map.203 = (bf16[16,16,128]{2,1,0:T(8,128)(2,1)}, f32[2,8,128]{2,1,0:T(8,128)S(1)}) custom-call(bf16[16,1024]{1,0:T(8,128)(2,1)} %tokens_hbm.1, f32[1,1024]{1,0:T(1,128)} %bitcast.30, bf16[192,1024]{1,0:T(8,128)(2,1)} %bitcast.23, f32[8,128]{1,0:T(8,128)} %bitcast.31), custom_call_target="tpu_custom_call" | custom-call | tf_op jit(solution)/shard_map/pallas_call | solution.py:455
  9.2 15.8 %all-to-all-start = ((bf16[16,16,128]{2,1,0:T(8,128)(2,1)}), bf16[16,16,128]{2,1,0:T(8,128)(2,1)S(1)}, u32[]{:S(2)}, u32[]{:S(2)}) async-start(bf16[16,16,128]{2,1,0:T(8,128)(2,1)} %get-tuple-element.27), calls=%async_computation | async-start | bytes 131072 | tf_op jit(solution)/shard_map/all_to_all | solution.py:466
  24.9 0.0 all-gather.3.cloned.1.call-start
  25.0 1.9 %shard_map.202 = (s32[4,16,128]{2,1,0:T(8,128)S(1)}, s32[8,128]{1,0:T(8,128)S(1)}, f32[8,128]{1,0:T(8,128)S(1)}, bf16[16,128,256]{2,1,0:T(8,128)(2,1)S(1)}, bf16...) custom-call(s32[16]{0:T(128)} %lengths_hbm.1, ...), custom_call_target="tpu_custom_call" | custom-call | tf_op jit(solution)/shard_map/pallas_call | solution.py:470
  26.9 9.6 %all-to-all-done.recv = bf16[16,16,128]{2,1,0:T(8,128)(2,1)S(1)} async-done(((bf16[16,16,128]{2,1,0:T(8,128)(2,1)}), bf16[16,16,128]{2,1,0:T(8,128)(2,1)S(1)}, u32[]{:S(2)}, u32[]{:S(2)}) %all-to-all-start) | async-done | bytes 65568 | tf_op jit(solution)/shard_map/all_to_all | solution.py:466
  36.5 1.8 %shard_map.204 = (f32[16,128]{1,0:T(8,128)S(1)}, f32[16,128]{1,0:T(8,128)S(1)}, bf16[328,256]{1,0:T(8,128)(2,1)}) custom-call(s32[1,2]{1,0:T(1,128)} %slots_hbm.5, s32[1,2]{1,0:T(1,128)} %dests_hbm.1, s32[2,16]{1,0:T(2,128)} %bitcast.28, bf16[16,16,128]{2,1,0:T(8,128)(2,1)S(1)} %all-to-all-done.recv, s32[4,16,128]{2,1,0:T(8,128)S(1)} %get-tuple-element.28.columns, ...), custom_call_target="tpu_custom_call" | custom-call | tf_op jit(solution)/shard_map/pallas_call | solution.py:504
  38.3 0.0 all-gather.3.cloned.1.call-update
  38.4 3.7 %collective-permute-start = (f32[16,128]{1,0:T(8,128)S(1)}, f32[16,128]{1,0:T(8,128)S(1)}, u32[]{:S(2)}, u32[]{:S(2)}) collective-permute-start(f32[16,128]{1,0:T(8,128)S(1)} %get-tuple-element.34), channel_id=1, source_target_pairs={{0,8},{1,9},{2,10},{3,11},{4,12},{5,13},{6,14},{7,15},{8,0},{9,1},... | collective-permute-start | bytes 24584 | tf_op jit(solution)/shard_map/ppermute | solution.py:519
  42.1 2.1 %shard_map.205 = (f32[16,64,128]{2,1,0:T(8,128)}, f32[16,128]{1,0:T(8,128)S(1)}, bf16[16,128,256]{2,1,0:T(8,128)(2,1)}) custom-call(bf16[16,16,128]{2,1,0:T(8,128)(2,1)S(1)} %all-to-all-done.recv, s32[4,16,128]{2,1,0:T(8,128)S(1)} %get-tuple-element.28.columns, f32[8,128]{1,0:T(8,128)S(1)} %get-tuple-element.29.rates, ...), custom_call_target="tpu_custom_call" | custom-call | tf_op jit(solution)/shard_map/pallas_call | solution.py:520
  44.1 7.3 %collective-permute-done.away = f32[16,128]{1,0:T(8,128)S(1)} collective-permute-done((f32[16,128]{1,0:T(8,128)S(1)}, f32[16,128]{1,0:T(8,128)S(1)}, u32[]{:S(2)}, u32[]{:S(2)}) %collective-permute-start) | collective-permute-done | bytes 8224 | tf_op jit(solution)/shard_map/ppermute | solution.py:519
  51.5 0.3 shard_map.206
  51.7 14.4 %all_to_all.30.recv = bf16[16,8,128]{2,1,0:T(8,128)(2,1)S(1)} all-to-all(bf16[16,8,128]{2,1,0:T(8,128)(2,1)S(1)} %shard_map.206), channel_id=1, replica_groups=mesh['rep'=32,'tp'=16] {'tp'}, dimensions={0} | all-to-all | bytes 65536 | tf_op jit(solution)/shard_map/all_to_all | solution.py:532
  66.2 0.1 shard_map.207
  66.3 14.0 %all_to_all.31.recv = bf16[16,8,128]{2,1,0:T(8,128)(2,1)S(1)} all-to-all(bf16[16,8,128]{2,1,0:T(8,128)(2,1)S(1)} %get-tuple-element.38), channel_id=1, replica_groups=mesh['rep'=32,'tp'=16] {'tp'}, dimensions={0} | all-to-all | bytes 65536 | tf_op jit(solution)/shard_map/all_to_all | solution.py:539
  80.2 0.5 shard_map.208
  80.7 14.0 %all_to_all.32.recv = bf16[16,8,128]{2,1,0:T(8,128)(2,1)S(1)} all-to-all(bf16[16,8,128]{2,1,0:T(8,128)(2,1)S(1)} %shard_map.208), channel_id=1, replica_groups=mesh['rep'=32,'tp'=16] {'tp'}, dimensions={0} | all-to-all | bytes 65536 | tf_op jit(solution)/shard_map/all_to_all | solution.py:544
  94.7 13.8 %all_to_all.33.recv.rows_all = bf16[16,8,128]{2,1,0:T(8,128)(2,1)S(1)} all-to-all(bf16[16,8,128]{2,1,0:T(8,128)(2,1)S(1)} %shard_map.209), channel_id=1, replica_groups=mesh['rep'=32,'tp'=16] {'tp'}, dimensions={0} | all-to-all | bytes 65536 | tf_op jit(solution)/shard_map/all_to_all | solution.py:547
  108.6 0.7 shard_map.210
  109.3 15.1 %all-to-all-start.5 = ((bf16[32,16,128]{2,1,0:T(8,128)(2,1)}), bf16[32,16,128]{2,1,0:T(8,128)(2,1)S(1)}, u32[]{:S(2)}, u32[]{:S(2)}) async-start(bf16[32,16,128]{2,1,0:T(8,128)(2,1)} %shard_map.210), calls=%async_computation.5 | async-start | bytes 262144 | tf_op jit(solution)/shard_map/all_to_all | solution.py:550
  124.4 0.0 all-gather.3.cloned.1.call-done
  124.4 2.7 %shard_map.211 = (bf16[16,128,256]{2,1,0:T(8,128)(2,1)}, f32[16,64,128]{2,1,0:T(8,128)}, f32[32,8,128]{2,1,0:T(8,128)S(1)}) custom-call(s32[2,16]{1,0:T(2,128)} %bitcast.29, s32[1,2]{1,0:T(1,128)} %slots_hbm.5, bf16[16,128,256]{2,1,0:T(8,128)(2,1)} %get-tuple-element.43.pool, ...), custom_call_target="tpu_custom_call", output_to_operand_aliasing={{0}: (2, {}), {1}: (3, {})} | custom-call | tf_op jit(solution)/shard_map/pallas_call | solution.py:552
  127.2 4.9 %all-to-all-done.5.recv = bf16[32,16,128]{2,1,0:T(8,128)(2,1)S(1)} async-done(((bf16[32,16,128]{2,1,0:T(8,128)(2,1)}), bf16[32,16,128]{2,1,0:T(8,128)(2,1)S(1)}, u32[]{:S(2)}, u32[]{:S(2)}) %all-to-all-start.5) | async-done | bytes 131104 | tf_op jit(solution)/shard_map/all_to_all | solution.py:550
  132.0 0.8 shard_map.212
  (1 shorter events, 0.0 us)
Async XLA Ops:
  9.2 27.3 %all-to-all-start = ((bf16[16,16,128]{2,1,0:T(8,128)(2,1)}), bf16[16,16,128]{2,1,0:T(8,128)(2,1)S(1)}, u32[]{:S(2)}, u32[]{:S(2)}) async-start(bf16[16,16,128]{2,1,0:T(8,128)(2,1)} %get-tuple-element.27), calls=%async_computation | async-start | bytes 131072 | tf_op jit(solution)/shard_map/all_to_all | solution.py:466
  24.9 99.5 %all-gather.3.cloned.1.call-start = ((), (), s32[]{:S(2)}) async-start(), calls=%async_computation.6 | async-start | bytes 5541888 | tf_op jit(solution)/shard_map/all_gather | solution.py:518
  38.4 13.1 %collective-permute-start = (f32[16,128]{1,0:T(8,128)S(1)}, f32[16,128]{1,0:T(8,128)S(1)}, u32[]{:S(2)}, u32[]{:S(2)}) collective-permute-start(f32[16,128]{1,0:T(8,128)S(1)} %get-tuple-element.34), channel_id=1, source_target_pairs={{0,8},{1,9},{2,10},{3,11},{4,12},{5,13},{6,14},{7,15},{8,0},{9,1},... | collective-permute-start | bytes 24584 | tf_op jit(solution)/shard_map/ppermute | solution.py:519
  109.3 22.8 %all-to-all-start.5 = ((bf16[32,16,128]{2,1,0:T(8,128)(2,1)}), bf16[32,16,128]{2,1,0:T(8,128)(2,1)S(1)}, u32[]{:S(2)}, u32[]{:S(2)}) async-start(bf16[32,16,128]{2,1,0:T(8,128)(2,1)} %shard_map.210), calls=%async_computation.5 | async-start | bytes 262144 | tf_op jit(solution)/shard_map/all_to_all | solution.py:550
Sparse Core Ops, SparseCore 0:
  38.5 57.0 all-gather.2

commit v4 on v3

--- a/solution.py
+++ b/solution.py
@@ -53,14 +53,17 @@
 
 
 def qkv_kernel(
-    tokens_hbm, gain_hbm, weight_hbm, mlp_gain_hbm, out, kept, tokens, gain, weight, sems
+    tokens_hbm, gain_hbm, weight_hbm, mlp_gain_hbm, out, kept, slices, tokens, gain, weight, sems
 ):
     loads = [
         pltpu.make_async_copy(tokens_hbm, tokens, sems.at[0]),
         pltpu.make_async_copy(gain_hbm, gain, sems.at[1]),
-        pltpu.make_async_copy(weight_hbm, weight, sems.at[2]),
-        pltpu.make_async_copy(mlp_gain_hbm, kept.at[1], sems.at[3]),
+        pltpu.make_async_copy(mlp_gain_hbm, kept.at[1], sems.at[2]),
     ]
+    part_rows = weight.shape[0] // 4
+    for i in range(4):
+        part = pl.ds(i * part_rows, part_rows)
+        loads.append(pltpu.make_async_copy(weight_hbm.at[part], weight.at[part], sems.at[3 + i]))
     for load in loads:
         load.start()
     t = lax.axis_index("tp")
@@ -69,9 +72,14 @@
     x = tokens[...].astype(f32)
     row = jnp.sum(jnp.where(row_ids(x.shape) == t, x, 0.0), axis=0, keepdims=True)
     kept[0] = jnp.concatenate([row[:, k * LANES : (k + 1) * LANES] for k in range(8)], axis=0)
+    mine = jnp.zeros(slices.shape, f32)
+    for k in range(8):
+        mine = jnp.where(t // 2 == k, x[:, k * LANES : (k + 1) * LANES], mine)
+    slices[...] = jnp.where(lax.rem(t, 2) == 1, mine, half_swap(mine))
     scale = lax.rsqrt(jnp.mean(x * x, axis=-1, keepdims=True) + 1e-05)
     normed = (x * scale * gain[...]).astype(bf16)
-    loads[2].wait()
+    for load in loads[3:]:
+        load.wait()
     part = lax.dot_general(normed, weight[...], NT, preferred_element_type=f32)
     part = part.astype(bf16).astype(f32)
     first = part[:, :LANES]
@@ -95,20 +103,20 @@
             slot = slot + jnp.where(mine, placed[j], 0.0)
         out[head] = slot.astype(bf16)
         out[head + 8] = slot.astype(bf16)
-    loads[3].wait()
+    loads[2].wait()
 
 
 def load_kernel(
-    lengths_hbm, groups_hbm, span_hbm, pages_hbm, slots_hbm, forget_hbm, rate_hbm,
+    lengths_hbm, groups_hbm, span_hbm, pages_hbm, slots_hbm, dests_hbm, forget_hbm, rate_hbm,
     pool_hbm, prefix_hbm, memory_hbm, weight_hbm, gate_hbm, up_hbm, down_hbm,
-    columns, marks, rates, pool, prefix, memory, weight, gate, up, down,
-    lengths, groups, span, pages, slots, forget, rate, small_sems, sems,
+    columns, marks, rates, pool, prefix, memory, weight, gate, up, down, leaving, send_out,
+    lengths, groups, span, pages, slots, dests, forget, rate, code, small_sems, sems, out_sems,
 ):
     small = [
         pltpu.make_async_copy(src, dst, small_sems.at[i])
         for i, (src, dst) in enumerate((
             (lengths_hbm, lengths), (groups_hbm, groups), (span_hbm, span), (pages_hbm, pages),
-            (slots_hbm, slots), (forget_hbm, forget), (rate_hbm, rate),
+            (slots_hbm, slots), (dests_hbm, dests), (forget_hbm, forget), (rate_hbm, rate),
         ))
     ]
     big = [
@@ -131,10 +139,29 @@
     columns[2] = column(lambda r: pages[half, r], rows)
     columns[3] = column(lambda r: span[r], rows)
     mark_row = row_ids(marks.shape)
-    marks[...] = jnp.where(mark_row == 0, slots[0, 0], slots[0, 1])
+    first = jnp.where(mark_row == 0, slots[0, 0], slots[0, 1])
+    second = jnp.where(mark_row == 2, dests[0, 0], dests[0, 1])
+    marks[...] = jnp.where(mark_row < 2, first, second)
     rates[...] = jnp.where(mark_row == 0, forget[head], rate[head])
-    for load in big:
+    dest = jnp.where(row_ids(code.shape) == 0, dests[0, 0], dests[0, 1])
+    code[...] = dest.astype(f32).astype(bf16)
+    big[0].wait()
+    stores = [
+        pltpu.make_async_copy(code, send_out.at[pl.ds(2 * LANES + 64, 8)], out_sems.at[0])
+    ]
+    for m in range(2):
+        page = pool.at[pages[half, slots[0, m]]]
+        block = send_out.at[pl.ds(m * LANES, LANES)]
+        stores.append(pltpu.make_async_copy(page, block, out_sems.at[1 + m]))
+    for store in stores:
+        store.start()
+    big[2].wait()
+    for m in range(2):
+        leaving[m] = memory[slots[0, m]]
+    for load in big[1:2] + big[3:]:
         load.wait()
+    for store in stores:
+        store.wait()
 
 
 def pick(recv, kind, head):
@@ -146,17 +173,11 @@
 
 
 def attend_kernel(
-    slots_hbm, dests_hbm, pages_hbm, recv, columns, rates, pool, prefix, memory,
+    recv, columns, rates, marks, pool, prefix, leaving, send_in,
     away_out, here_out, send_out,
-    slots, dests, pages, small_sems,
+    moving, send_sem,
 ):
-    small = [
-        pltpu.make_async_copy(slots_hbm, slots, small_sems.at[0]),
-        pltpu.make_async_copy(dests_hbm, dests, small_sems.at[1]),
-        pltpu.make_async_copy(pages_hbm, pages, small_sems.at[2]),
-    ]
-    for load in small:
-        load.start()
+    del send_in
     t = lax.axis_index("tp")
     half = t // 8
     head = lax.rem(t, 8)
@@ -166,6 +187,24 @@
     rows = query.shape[0]
     lanes = lane_ids((rows, LANES))
     low = lanes < 64
+    key_unit = key * lax.rsqrt(jnp.sum(key * key, axis=-1, keepdims=True) + 1e-06)
+    value_half = jnp.where(half == 0, value, half_swap(value))
+    row = row_ids(lanes.shape)
+    mem_shape = leaving.shape[1:]
+    diagonal = row_ids(mem_shape) == lane_ids(mem_shape)
+    for m in range(2):
+        mine = row == marks[m : m + 1]
+        key_row = jnp.sum(jnp.where(mine, key_unit, 0.0), axis=0, keepdims=True)
+        value_row = jnp.sum(jnp.where(mine, value_half, 0.0), axis=0, keepdims=True)
+        closes = jnp.max(jnp.where(mine, columns[3], 0), axis=0, keepdims=True) == 1
+        block = leaving[m]
+        seen = jnp.sum(block * key_row, axis=1, keepdims=True)
+        target = jnp.sum(jnp.where(diagonal, value_row, 0.0), axis=1, keepdims=True)
+        written = rates[0:1] * block + rates[1:2] * (target - seen) * key_row
+        written = jnp.where(closes, written, block)
+        moving[:, m * LANES : (m + 1) * LANES] = written.astype(bf16)
+    send = pltpu.make_async_copy(moving, send_out.at[pl.ds(2 * LANES, 64)], send_sem)
+    send.start()
     length = columns[0]
     group = columns[1]
     page = columns[2]
@@ -218,30 +257,7 @@
     swapped = half_swap(attended)
     here_out[...] = jnp.where(low, jnp.where(half == 0, attended, swapped), lse)
     away_out[...] = jnp.where(low, jnp.where(half == 0, swapped, attended), lse)
-
-    key_unit = key * lax.rsqrt(jnp.sum(key * key, axis=-1, keepdims=True) + 1e-06)
-    value_half = jnp.where(half == 0, value, half_swap(value))
-    closing = columns[3]
-    row = row_ids(lanes.shape)
-    mem_shape = memory.shape[1:]
-    diagonal = row_ids(mem_shape) == lane_ids(mem_shape)
-    for load in small:
-        load.wait()
-    for m in range(2):
-        slot = slots[0, m]
-        mine = row == slot
-        key_row = jnp.sum(jnp.where(mine, key_unit, 0.0), axis=0, keepdims=True)
-        value_row = jnp.sum(jnp.where(mine, value_half, 0.0), axis=0, keepdims=True)
-        closes = jnp.max(jnp.where(mine, closing, 0), axis=0, keepdims=True) == 1
-        block = memory[slot]
-        seen = jnp.sum(block * key_row, axis=1, keepdims=True)
-        target = jnp.sum(jnp.where(diagonal, value_row, 0.0), axis=1, keepdims=True)
-        written = rates[0:1] * block + rates[1:2] * (target - seen) * key_row
-        written = jnp.where(closes, written, block)
-        send_out[m * LANES : (m + 1) * LANES, :] = pool[pages[half, slot]]
-        send_out[2 * LANES : 2 * LANES + 64, m * LANES : (m + 1) * LANES] = written.astype(bf16)
-    code = jnp.where(row_ids((8, 2 * LANES)) == 0, dests[0, 0], dests[0, 1])
-    send_out[2 * LANES + 64 :, :] = code.astype(f32).astype(bf16)
+    send.wait()
 
 
 def memory_kernel(
@@ -296,7 +312,7 @@
         rows[:, k, :] = wide[:, k * LANES : (k + 1) * LANES]
 
 
-def project_kernel(here, away, recalled, weight, out, rows):
+def join_kernel(here, away, recalled, slices, marks, mixed_out, out):
     mine = here[...]
     other = away[...]
     lse = mine[:, 64:65]
@@ -304,13 +320,45 @@
     share = 1.0 / (1.0 + jnp.exp(lse_other - lse))
     share_other = 1.0 / (1.0 + jnp.exp(lse - lse_other))
     mixed = share * mine + share_other * other + recalled[...]
-    mixed = mixed.astype(bf16)[:, :64]
-    spread(rows, jnp.dot(mixed, weight[...], preferred_element_type=f32))
+    mixed = jnp.where(lane_ids(mixed.shape) < 64, mixed, slices[...])
+    mixed_out[...] = mixed
+    row = row_ids(mixed.shape)
+    parts = []
+    for m in range(2):
+        parts.append(jnp.sum(jnp.where(row == marks[m : m + 1], mixed, 0.0), axis=0, keepdims=True))
+    parts.append(marks[2:8].astype(f32))
+    block = jnp.concatenate(parts, axis=0).astype(bf16)
+    for s in range(out.shape[0]):
+        out[s] = block
+
+
+def project_kernel(mixed_in, arrived, marks, weight, out, rows, came):
+    t = lax.axis_index("tp")
+    me = lax.axis_index("rep").astype(f32)
+    came[...] = arrived[...].astype(f32)
+    mixed = mixed_in[...]
+    row = row_ids(mixed.shape)
+    extra = jnp.zeros(mixed.shape, f32)
+    for m in range(2):
+        match = came[:, 2 + m, :] == me
+        entry = jnp.sum(jnp.where(match, came[:, m, :], 0.0), axis=0, keepdims=True)
+        here = row == marks[m : m + 1]
+        mixed = jnp.where(here, entry, mixed)
+        extra = jnp.where(here, entry, extra)
+    low = lane_ids(extra.shape) < 64
+    odd = lax.rem(t, 2) == 1
+    extra = jnp.where(low, jnp.where(odd, 0.0, half_swap(extra)), jnp.where(odd, extra, 0.0))
+    wide = jnp.dot(mixed.astype(bf16)[:, :64], weight[...], preferred_element_type=f32)
+    for k in range(8):
+        tile = wide[:, k * LANES : (k + 1) * LANES]
+        rows[:, k, :] = tile + jnp.where(t // 2 == k, extra, 0.0)
     out[...] = rows[...].astype(bf16)
 
 
-def hidden_kernel(recv, kept, hidden_out, normed_out):
-    hidden = kept[0]
+def hidden_kernel(recv, kept, marks, hidden_out, normed_out):
+    t = lax.axis_index("tp")
+    taken = (marks[0:1] == t) | (marks[1:2] == t)
+    hidden = jnp.where(taken, 0.0, kept[0])
     for s in range(recv.shape[0]):
         hidden = hidden + recv[s].astype(f32)
     hidden_out[...] = hidden
@@ -338,19 +386,6 @@
     row = total.astype(bf16)
     for s in range(16):
         out[s] = row
-
-
-def leave_kernel(marks, recv, out):
-    leaving = []
-    for m in range(2):
-        mark = marks[m : m + 1]
-        row = jnp.zeros(recv.shape[1:], f32)
-        for s in range(recv.shape[0]):
-            row = jnp.where(mark == s, recv[s].astype(f32), row)
-        leaving.append(row)
-    both = jnp.concatenate(leaving, axis=0).astype(bf16)
-    for s in range(out.shape[0]):
-        out[s] = both
 
 
 def place_kernel(
@@ -403,20 +438,9 @@
         store.wait()
 
 
-def rows_kernel(marks, rows_all, recv, codes, rows_out, rows):
-    me = lax.axis_index("rep").astype(f32)
-    arriving = []
-    for m in range(2):
-        row = jnp.zeros(rows_all.shape[1:], f32)
-        for s in range(recv.shape[0]):
-            part = recv[s, 8 * m : 8 * m + 8, :].astype(f32)
-            row = jnp.where(codes[s, m : m + 1, :] == me, part, row)
-        arriving.append(row)
-    for s in range(rows_all.shape[0]):
-        row = rows_all[s].astype(f32)
-        for m in range(2):
-            row = jnp.where(marks[m : m + 1] == s, arriving[m], row)
-        rows[s] = row
+def rows_kernel(rows_all, codes, rows_out, rows):
+    del codes
+    rows[...] = rows_all[...].astype(f32)
     for k in range(8):
         rows_out[:, k * LANES : (k + 1) * LANES] = rows[:, k, :].astype(bf16)
 
@@ -452,15 +476,19 @@
     mem = memory[:, 0]
     send_shape = shape((2 * LANES + 72, 2 * LANES), bf16)
 
-    qkv_slots, kept = call(
+    qkv_slots, kept, slices = call(
         qkv_kernel,
-        (shape((n_tp, rows, LANES), bf16), shape((2, 8, LANES), f32)),
+        (
+            shape((n_tp, rows, LANES), bf16),
+            shape((2, 8, LANES), f32),
+            shape((rows, LANES), f32),
+        ),
         [HBM] * 4,
         scratch=[
             pltpu.VMEM(tokens.shape, bf16),
             pltpu.VMEM((1, tokens.shape[1]), f32),
             pltpu.VMEM(qkv_weight.shape[::-1], bf16),
-            pltpu.SemaphoreType.DMA((4,)),
+            pltpu.SemaphoreType.DMA((7,)),
         ],
     )(*in_hbm(tokens, norm_attn.reshape(1, -1), qkv_weight.T, norm_mlp.reshape(8, LANES)))
     qkv_recv = lax.all_to_all(qkv_slots, "tp", 0, 0)
@@ -480,40 +508,42 @@
             shape(gate.shape, bf16),
             shape(up.shape, bf16),
             shape(down_weight.shape, bf16),
+            shape((2,) + mem.shape[1:], f32),
+            send_shape,
         ),
-        [HBM] * 14,
+        [HBM] * 15,
+        out_specs=(VMEM,) * 11 + (HBM,),
         scratch=[
             pltpu.SMEM((rows,), jnp.int32),
             pltpu.SMEM((rows,), jnp.int32),
             pltpu.SMEM((rows,), jnp.int32),
             pltpu.SMEM(pages.shape, jnp.int32),
             pltpu.SMEM(out_slot.shape, jnp.int32),
+            pltpu.SMEM(move_dest.shape, jnp.int32),
             pltpu.SMEM(forget.shape, f32),
             pltpu.SMEM(write_rate.shape, f32),
+            pltpu.VMEM((8, 2 * LANES), bf16),
+            pltpu.SemaphoreType.DMA((8,)),
             pltpu.SemaphoreType.DMA((7,)),
-            pltpu.SemaphoreType.DMA((7,)),
+            pltpu.SemaphoreType.DMA((3,)),
         ],
     )(
-        *in_hbm(lengths, prompt_group, span_close, pages, out_slot, forget, write_rate),
+        *in_hbm(lengths, prompt_group, span_close, pages, out_slot, move_dest, forget, write_rate),
         *in_hbm(pool, prefix, mem, out_weight, gate, up, down_weight),
     )
 
     columns, marks, rates, pool_near, prefix_near, mem_near = loaded[:6]
-    out_near, gate_near, up_near, down_near = loaded[6:]
+    out_near, gate_near, up_near, down_near, leaving_mem, send = loaded[6:]
 
     away, here, send = call(
         attend_kernel,
         (shape((rows, LANES), f32), shape((rows, LANES), f32), send_shape),
-        [HBM] * 3 + [VMEM] * 6,
-        scratch=[
-            pltpu.SMEM(out_slot.shape, jnp.int32),
-            pltpu.SMEM(move_dest.shape, jnp.int32),
-            pltpu.SMEM(pages.shape, jnp.int32),
-            pltpu.SemaphoreType.DMA((3,)),
-        ],
+        [VMEM] * 7 + [HBM],
+        out_specs=(VMEM, VMEM, HBM),
+        scratch=[pltpu.VMEM((64, 2 * LANES), bf16), pltpu.SemaphoreType.DMA],
+        aliases={7: 2},
     )(
-        *in_hbm(out_slot, move_dest, pages),
-        qkv_recv, columns, rates, pool_near, prefix_near, mem_near,
+        qkv_recv, columns, rates, marks, pool_near, prefix_near, leaving_mem, *in_hbm(send)
     )
     gathered = lax.all_gather(send, "rep", axis=0)
     away_recv = lax.ppermute(away, "tp", [(i, (i + n_tp // 2) % n_tp) for i in range(n_tp)])
@@ -526,16 +556,23 @@
     )(qkv_recv, columns, rates, pool_near, mem_near)
 
     row_scratch = pltpu.VMEM((rows, 8, LANES), f32)
+    mixed, leaving = call(
+        join_kernel, (shape((rows, LANES), f32), shape((n_rep, 8, LANES), bf16)), [VMEM] * 5
+    )(here, away_recv, recalled, slices, marks)
+    arrived = lax.all_to_all(leaving, "rep", 0, 0)
     terms = call(
-        project_kernel, shape((n_tp, 8, LANES), bf16), [VMEM] * 4, scratch=[row_scratch]
-    )(here, away_recv, recalled, out_near)
+        project_kernel,
+        shape((n_tp, 8, LANES), bf16),
+        [VMEM] * 4,
+        scratch=[row_scratch, pltpu.VMEM((n_rep, 8, LANES), f32)],
+    )(mixed, arrived, marks, out_near)
     terms_recv = lax.all_to_all(terms, "tp", 0, 0)
 
     hidden, normed_slots = call(
         hidden_kernel,
         (shape((8, LANES), f32), shape((n_tp, 8, LANES), bf16)),
-        [VMEM] * 2,
-    )(terms_recv, kept)
+        [VMEM] * 3,
+    )(terms_recv, kept, marks)
     normed_recv = lax.all_to_all(normed_slots, "tp", 0, 0)
 
     down_slots = call(
@@ -545,9 +582,6 @@
 
     row_slots = call(row_kernel, shape((n_tp, 8, LANES), bf16), [VMEM] * 2)(down_recv, hidden)
     rows_all = lax.all_to_all(row_slots, "tp", 0, 0)
-
-    leaving = call(leave_kernel, shape((n_rep, 16, LANES), bf16), [VMEM] * 2)(marks, rows_all)
-    arrived = lax.all_to_all(leaving, "rep", 0, 0)
 
     pool_out, mem_out, codes = call(
         place_kernel,
@@ -569,8 +603,8 @@
         aliases={2: 0, 3: 1},
     )(*in_hbm(pages, out_slot, pool_base, mem_after, gathered))
     rows_out = call(
-        rows_kernel, shape(tokens.shape, bf16), [VMEM] * 4, scratch=[row_scratch]
-    )(marks, rows_all, arrived, codes)
+        rows_kernel, shape(tokens.shape, bf16), [VMEM] * 2, scratch=[row_scratch]
+    )(rows_all, codes)
     return rows_out, mem_out[:, None], pool_out[:, None]
 
 

time: 140 us -> 138 us (0.986)
  the two profiles are of different devices: /device:TPU:1 before, /device:TPU:2 now
where the time goes in v4:
time: 138 us; the launch traced here: 137 us
  blocking collectives  59.5 us (43%)
  waiting for transfers between devices  28.5 us (21%)
  starting transfers between devices  22.3 us (16%)
  between operations  14.1 us (10%)
  Pallas kernels  12.3 us (9%)
    all_to_all x1, blocking collectives, body(): terms_recv = lax.all_to_all(terms, 'tp', 0, 0)  15.5 us
    all_to_all x1, starting transfers between devices, body(): qkv_recv = lax.all_to_all(qkv_slots, 'tp', 0, 0)  15.2 us
    all_to_all x1, blocking collectives, body(): down_recv = lax.all_to_all(down_slots, 'tp', 0, 0)  15.2 us
    all_to_all x1, blocking collectives, body(): normed_recv = lax.all_to_all(normed_slots, 'tp', 0, 0)  15.2 us
    all_to_all x1, blocking collectives, body(): arrived = lax.all_to_all(leaving, 'rep', 0, 0)  13.7 us
    all_to_all x1, waiting for transfers between devices, body(): qkv_recv = lax.all_to_all(qkv_slots, 'tp', 0, 0)  10 us
    all_to_all x1, waiting for transfers between devices, body(): rows_all = lax.all_to_all(row_slots, 'tp', 0, 0)  9.81 us
    ppermute x1, waiting for transfers between devices, body(): lax.ppermute(away, 'tp', [(i, (i + n_tp // 2) % n_tp) for i in range(n_tp)])  8.65 us
  transfers between devices with their start and end apart: 4, of which 3 were waited for; matrix products, arithmetic and copies ran while one was open for 0% of the time, Pallas kernels for 6%

profile of v4, /device:TPU:2, one launch (start us, length us, event | category | flops | bytes accessed | tf_op | source)
XLA Modules:
  0.0 137.4 jit_solution(10834278161038161430)
XLA Ops:
  7.2 2.1 %shard_map.202 = (bf16[16,16,128]{2,1,0:T(8,128)(2,1)}, f32[2,8,128]{2,1,0:T(8,128)S(1)}, f32[16,128]{1,0:T(8,128)S(1)}) custom-call(bf16[16,1024]{1,0:T(8,128)(2,1)} %tokens_hbm.1, f32[1,1024]{1,0:T(1,128)} %bitcast.29, bf16[192,1024]{1,0:T(8,128)(2,1)} %bitcast.23, f32[8,128]{1,0:T(8,128)} %bitcast.30), custom_call_target="tpu_custom_call" | custom-call | tf_op jit(solution)/shard_map/pallas_call | solution.py:479
  9.3 15.2 %all-to-all-start = ((bf16[16,16,128]{2,1,0:T(8,128)(2,1)}), bf16[16,16,128]{2,1,0:T(8,128)(2,1)S(1)}, u32[]{:S(2)}, u32[]{:S(2)}) async-start(bf16[16,16,128]{2,1,0:T(8,128)(2,1)} %get-tuple-element.31), calls=%async_computation | async-start | bytes 131072 | tf_op jit(solution)/shard_map/all_to_all | solution.py:494
  24.5 0.0 all-gather.3.cloned.1.call-start
  24.5 2.0 %shard_map.203 = (s32[4,16,128]{2,1,0:T(8,128)S(1)}, s32[8,128]{1,0:T(8,128)S(1)}, f32[8,128]{1,0:T(8,128)S(1)}, bf16[16,128,256]{2,1,0:T(8,128)(2,1)S(1)}, bf16...) custom-call(s32[16]{0:T(128)} %lengths_hbm.1, ...), custom_call_target="tpu_custom_call" | custom-call | tf_op jit(solution)/shard_map/pallas_call | solution.py:498
  26.5 0.0 copy-start
  26.5 0.7 copy-done
  27.2 10.0 %all-to-all-done.recv = bf16[16,16,128]{2,1,0:T(8,128)(2,1)S(1)} async-done(((bf16[16,16,128]{2,1,0:T(8,128)(2,1)}), bf16[16,16,128]{2,1,0:T(8,128)(2,1)S(1)}, u32[]{:S(2)}, u32[]{:S(2)}) %all-to-all-start) | async-done | bytes 65568 | tf_op jit(solution)/shard_map/all_to_all | solution.py:494
  37.2 1.1 shard_map.204
  38.4 0.0 all-gather.3.cloned.1.call-update
  38.4 3.5 %collective-permute-start = (f32[16,128]{1,0:T(8,128)S(1)}, f32[16,128]{1,0:T(8,128)S(1)}, u32[]{:S(2)}, u32[]{:S(2)}) collective-permute-start(f32[16,128]{1,0:T(8,128)S(1)} %get-tuple-element.40), channel_id=1, source_target_pairs={{0,8},{1,9},{2,10},{3,11},{4,12},{5,13},{6,14},{7,15},{8,0},{9,1},... | collective-permute-start | bytes 24584 | tf_op jit(solution)/shard_map/ppermute | solution.py:549
  41.9 2.1 %shard_map.205 = (f32[16,64,128]{2,1,0:T(8,128)}, f32[16,128]{1,0:T(8,128)S(1)}, bf16[16,128,256]{2,1,0:T(8,128)(2,1)}) custom-call(bf16[16,16,128]{2,1,0:T(8,128)(2,1)S(1)} %all-to-all-done.recv, s32[4,16,128]{2,1,0:T(8,128)S(1)} %get-tuple-element.32.columns, f32[8,128]{1,0:T(8,128)S(1)} %get-tuple-element.33.rates, ...), custom_call_target="tpu_custom_call" | custom-call | tf_op jit(solution)/shard_map/pallas_call | solution.py:550
  44.0 8.7 %collective-permute-done.away = f32[16,128]{1,0:T(8,128)S(1)} collective-permute-done((f32[16,128]{1,0:T(8,128)S(1)}, f32[16,128]{1,0:T(8,128)S(1)}, u32[]{:S(2)}, u32[]{:S(2)}) %collective-permute-start) | collective-permute-done | bytes 8224 | tf_op jit(solution)/shard_map/ppermute | solution.py:549
  52.6 0.1 shard_map.206
  52.7 13.7 %all_to_all.30.arrived = bf16[32,8,128]{2,1,0:T(8,128)(2,1)S(1)} all-to-all(bf16[32,8,128]{2,1,0:T(8,128)(2,1)S(1)} %get-tuple-element.45), channel_id=1, replica_groups=mesh['rep'=32,'tp'=16] {'rep'}, dimensions={0} | all-to-all | bytes 131072 | tf_op jit(solution)/shard_map/all_to_all | solution.py:562
  66.5 0.2 shard_map.207
  66.7 15.5 %all_to_all.31.recv = bf16[16,8,128]{2,1,0:T(8,128)(2,1)S(1)} all-to-all(bf16[16,8,128]{2,1,0:T(8,128)(2,1)S(1)} %shard_map.207), channel_id=1, replica_groups=mesh['rep'=32,'tp'=16] {'tp'}, dimensions={0} | all-to-all | bytes 65536 | tf_op jit(solution)/shard_map/all_to_all | solution.py:569
  82.2 0.1 shard_map.208
  82.3 15.2 %all_to_all.32.recv = bf16[16,8,128]{2,1,0:T(8,128)(2,1)S(1)} all-to-all(bf16[16,8,128]{2,1,0:T(8,128)(2,1)S(1)} %get-tuple-element.48), channel_id=1, replica_groups=mesh['rep'=32,'tp'=16] {'tp'}, dimensions={0} | all-to-all | bytes 65536 | tf_op jit(solution)/shard_map/all_to_all | solution.py:576
  97.5 0.5 shard_map.209
  98.0 15.2 %all_to_all.33.recv = bf16[16,8,128]{2,1,0:T(8,128)(2,1)S(1)} all-to-all(bf16[16,8,128]{2,1,0:T(8,128)(2,1)S(1)} %shard_map.209), channel_id=1, replica_groups=mesh['rep'=32,'tp'=16] {'tp'}, dimensions={0} | all-to-all | bytes 65536 | tf_op jit(solution)/shard_map/all_to_all | solution.py:581
  113.1 0.6 shard_map.210
  113.8 3.5 %all-to-all-start.5 = ((bf16[16,8,128]{2,1,0:T(8,128)(2,1)}), bf16[16,8,128]{2,1,0:T(8,128)(2,1)S(1)}, u32[]{:S(2)}, u32[]{:S(2)}) async-start(bf16[16,8,128]{2,1,0:T(8,128)(2,1)} %shard_map.210), calls=%async_computation.5 | async-start | bytes 65536 | tf_op jit(solution)/shard_map/all_to_all | solution.py:584
  117.3 0.0 all-gather.3.cloned.1.call-done
  117.3 2.7 %shard_map.211 = (bf16[16,128,256]{2,1,0:T(8,128)(2,1)}, f32[16,64,128]{2,1,0:T(8,128)}, f32[32,8,128]{2,1,0:T(8,128)S(1)}) custom-call(s32[2,16]{1,0:T(2,128)} %bitcast.28, s32[1,2]{1,0:T(1,128)} %slots_hbm.3, bf16[16,128,256]{2,1,0:T(8,128)(2,1)} %get-tuple-element.53.pool, ...), custom_call_target="tpu_custom_call", output_to_operand_aliasing={{0}: (2, {}), {1}: (3, {})} | custom-call | tf_op jit(solution)/shard_map/pallas_call | solution.py:586
  120.0 9.8 %all-to-all-done.5.rows_all = bf16[16,8,128]{2,1,0:T(8,128)(2,1)S(1)} async-done(((bf16[16,8,128]{2,1,0:T(8,128)(2,1)}), bf16[16,8,128]{2,1,0:T(8,128)(2,1)S(1)}, u32[]{:S(2)}, u32[]{:S(2)}) %all-to-all-start.5) | async-done | bytes 32800 | tf_op jit(solution)/shard_map/all_to_all | solution.py:584
  129.8 0.7 shard_map.212
Async XLA Ops:
  9.3 27.9 %all-to-all-start = ((bf16[16,16,128]{2,1,0:T(8,128)(2,1)}), bf16[16,16,128]{2,1,0:T(8,128)(2,1)S(1)}, u32[]{:S(2)}, u32[]{:S(2)}) async-start(bf16[16,16,128]{2,1,0:T(8,128)(2,1)} %get-tuple-element.31), calls=%async_computation | async-start | bytes 131072 | tf_op jit(solution)/shard_map/all_to_all | solution.py:494
  24.5 92.8 %all-gather.3.cloned.1.call-start = ((), (), s32[]{:S(2)}) async-start(), calls=%async_computation.6 | async-start | bytes 5541888 | tf_op jit(solution)/shard_map/all_gather | solution.py:548
  26.5 0.7 copy-start
  38.4 14.3 %collective-permute-start = (f32[16,128]{1,0:T(8,128)S(1)}, f32[16,128]{1,0:T(8,128)S(1)}, u32[]{:S(2)}, u32[]{:S(2)}) collective-permute-start(f32[16,128]{1,0:T(8,128)S(1)} %get-tuple-element.40), channel_id=1, source_target_pairs={{0,8},{1,9},{2,10},{3,11},{4,12},{5,13},{6,14},{7,15},{8,0},{9,1},... | collective-permute-start | bytes 24584 | tf_op jit(solution)/shard_map/ppermute | solution.py:549
  113.8 16.1 %all-to-all-start.5 = ((bf16[16,8,128]{2,1,0:T(8,128)(2,1)}), bf16[16,8,128]{2,1,0:T(8,128)(2,1)S(1)}, u32[]{:S(2)}, u32[]{:S(2)}) async-start(bf16[16,8,128]{2,1,0:T(8,128)(2,1)} %shard_map.210), calls=%async_computation.5 | async-start | bytes 65536 | tf_op jit(solution)/shard_map/all_to_all | solution.py:584
Sparse Core Ops, SparseCore 0:
  38.5 54.8 all-gather.2

commit v5 on v4

--- a/solution.py
+++ b/solution.py
@@ -60,10 +60,10 @@
         pltpu.make_async_copy(gain_hbm, gain, sems.at[1]),
         pltpu.make_async_copy(mlp_gain_hbm, kept.at[1], sems.at[2]),
     ]
-    part_rows = weight.shape[0] // 4
+    width = weight.shape[2]
     for i in range(4):
-        part = pl.ds(i * part_rows, part_rows)
-        loads.append(pltpu.make_async_copy(weight_hbm.at[part], weight.at[part], sems.at[3 + i]))
+        piece = weight_hbm.at[:, pl.ds(i * width, width)]
+        loads.append(pltpu.make_async_copy(piece, weight.at[i], sems.at[3 + i]))
     for load in loads:
         load.start()
     t = lax.axis_index("tp")
@@ -78,9 +78,11 @@
     slices[...] = jnp.where(lax.rem(t, 2) == 1, mine, half_swap(mine))
     scale = lax.rsqrt(jnp.mean(x * x, axis=-1, keepdims=True) + 1e-05)
     normed = (x * scale * gain[...]).astype(bf16)
-    for load in loads[3:]:
-        load.wait()
-    part = lax.dot_general(normed, weight[...], NT, preferred_element_type=f32)
+    part = jnp.zeros((x.shape[0], weight.shape[1]), f32)
+    for i in range(4):
+        loads[3 + i].wait()
+        cut = normed[:, i * width : (i + 1) * width]
+        part = part + lax.dot_general(cut, weight[i], NT, preferred_element_type=f32)
     part = part.astype(bf16).astype(f32)
     first = part[:, :LANES]
     last = part[:, LANES:]
@@ -487,7 +489,7 @@
         scratch=[
             pltpu.VMEM(tokens.shape, bf16),
             pltpu.VMEM((1, tokens.shape[1]), f32),
-            pltpu.VMEM(qkv_weight.shape[::-1], bf16),
+            pltpu.VMEM((4, qkv_weight.shape[1], qkv_weight.shape[0] // 4), bf16),
             pltpu.SemaphoreType.DMA((7,)),
         ],
     )(*in_hbm(tokens, norm_attn.reshape(1, -1), qkv_weight.T, norm_mlp.reshape(8, LANES)))

time: 138 us -> 138 us (level)
  no operation moved by 1% of the time
where the time goes in v5:
time: 138 us; the launch traced here: 137 us
  blocking collectives  59.5 us (43%)
  waiting for transfers between devices  28.5 us (21%)
  starting transfers between devices  22.3 us (16%)
  between operations  14.1 us (10%)
  Pallas kernels  12.4 us (9%)
    all_to_all x1, blocking collectives, body(): terms_recv = lax.all_to_all(terms, 'tp', 0, 0)  15.5 us
    all_to_all x1, starting transfers between devices, body(): qkv_recv = lax.all_to_all(qkv_slots, 'tp', 0, 0)  15.2 us
    all_to_all x1, blocking collectives, body(): down_recv = lax.all_to_all(down_slots, 'tp', 0, 0)  15.2 us
    all_to_all x1, blocking collectives, body(): normed_recv = lax.all_to_all(normed_slots, 'tp', 0, 0)  15.2 us
    all_to_all x1, blocking collectives, body(): arrived = lax.all_to_all(leaving, 'rep', 0, 0)  13.7 us
    all_to_all x1, waiting for transfers between devices, body(): qkv_recv = lax.all_to_all(qkv_slots, 'tp', 0, 0)  10 us
    all_to_all x1, waiting for transfers between devices, body(): rows_all = lax.all_to_all(row_slots, 'tp', 0, 0)  9.81 us
    ppermute x1, waiting for transfers between devices, body(): lax.ppermute(away, 'tp', [(i, (i + n_tp // 2) % n_tp) for i in range(n_tp)])  8.65 us
  transfers between devices with their start and end apart: 4, of which 3 were waited for; matrix products, arithmetic and copies ran while one was open for 0% of the time, Pallas kernels for 6%

profile of v5, /device:TPU:2, one launch (start us, length us, event | category | flops | bytes accessed | tf_op | source)
XLA Modules:
  0.0 137.5 jit_solution(12625785825688656717)
XLA Ops:
  7.2 2.2 %shard_map.202 = (bf16[16,16,128]{2,1,0:T(8,128)(2,1)}, f32[2,8,128]{2,1,0:T(8,128)S(1)}, f32[16,128]{1,0:T(8,128)S(1)}) custom-call(bf16[16,1024]{1,0:T(8,128)(2,1)} %tokens_hbm.1, f32[1,1024]{1,0:T(1,128)} %bitcast.29, bf16[192,1024]{1,0:T(8,128)(2,1)} %bitcast.23, f32[8,128]{1,0:T(8,128)} %bitcast.30), custom_call_target="tpu_custom_call" | custom-call | tf_op jit(solution)/shard_map/pallas_call | solution.py:481
  9.4 15.2 %all-to-all-start = ((bf16[16,16,128]{2,1,0:T(8,128)(2,1)}), bf16[16,16,128]{2,1,0:T(8,128)(2,1)S(1)}, u32[]{:S(2)}, u32[]{:S(2)}) async-start(bf16[16,16,128]{2,1,0:T(8,128)(2,1)} %get-tuple-element.31), calls=%async_computation | async-start | bytes 131072 | tf_op jit(solution)/shard_map/all_to_all | solution.py:496
  24.6 0.0 all-gather.3.cloned.1.call-start
  24.7 2.0 %shard_map.203 = (s32[4,16,128]{2,1,0:T(8,128)S(1)}, s32[8,128]{1,0:T(8,128)S(1)}, f32[8,128]{1,0:T(8,128)S(1)}, bf16[16,128,256]{2,1,0:T(8,128)(2,1)S(1)}, bf16...) custom-call(s32[16]{0:T(128)} %lengths_hbm.1, ...), custom_call_target="tpu_custom_call" | custom-call | tf_op jit(solution)/shard_map/pallas_call | solution.py:500
  26.6 0.0 copy-start
  26.6 0.7 copy-done
  27.3 10.0 %all-to-all-done.recv = bf16[16,16,128]{2,1,0:T(8,128)(2,1)S(1)} async-done(((bf16[16,16,128]{2,1,0:T(8,128)(2,1)}), bf16[16,16,128]{2,1,0:T(8,128)(2,1)S(1)}, u32[]{:S(2)}, u32[]{:S(2)}) %all-to-all-start) | async-done | bytes 65568 | tf_op jit(solution)/shard_map/all_to_all | solution.py:496
  37.3 1.1 shard_map.204
  38.5 0.0 all-gather.3.cloned.1.call-update
  38.5 3.5 %collective-permute-start = (f32[16,128]{1,0:T(8,128)S(1)}, f32[16,128]{1,0:T(8,128)S(1)}, u32[]{:S(2)}, u32[]{:S(2)}) collective-permute-start(f32[16,128]{1,0:T(8,128)S(1)} %get-tuple-element.40), channel_id=1, source_target_pairs={{0,8},{1,9},{2,10},{3,11},{4,12},{5,13},{6,14},{7,15},{8,0},{9,1},... | collective-permute-start | bytes 24584 | tf_op jit(solution)/shard_map/ppermute | solution.py:551
  42.1 2.1 %shard_map.205 = (f32[16,64,128]{2,1,0:T(8,128)}, f32[16,128]{1,0:T(8,128)S(1)}, bf16[16,128,256]{2,1,0:T(8,128)(2,1)}) custom-call(bf16[16,16,128]{2,1,0:T(8,128)(2,1)S(1)} %all-to-all-done.recv, s32[4,16,128]{2,1,0:T(8,128)S(1)} %get-tuple-element.32.columns, f32[8,128]{1,0:T(8,128)S(1)} %get-tuple-element.33.rates, ...), custom_call_target="tpu_custom_call" | custom-call | tf_op jit(solution)/shard_map/pallas_call | solution.py:552
  44.1 8.7 %collective-permute-done.away = f32[16,128]{1,0:T(8,128)S(1)} collective-permute-done((f32[16,128]{1,0:T(8,128)S(1)}, f32[16,128]{1,0:T(8,128)S(1)}, u32[]{:S(2)}, u32[]{:S(2)}) %collective-permute-start) | collective-permute-done | bytes 8224 | tf_op jit(solution)/shard_map/ppermute | solution.py:551
  52.8 0.1 shard_map.206
  52.9 13.7 %all_to_all.30.arrived = bf16[32,8,128]{2,1,0:T(8,128)(2,1)S(1)} all-to-all(bf16[32,8,128]{2,1,0:T(8,128)(2,1)S(1)} %get-tuple-element.45), channel_id=1, replica_groups=mesh['rep'=32,'tp'=16] {'rep'}, dimensions={0} | all-to-all | bytes 131072 | tf_op jit(solution)/shard_map/all_to_all | solution.py:564
  66.6 0.2 shard_map.207
  66.8 15.5 %all_to_all.31.recv = bf16[16,8,128]{2,1,0:T(8,128)(2,1)S(1)} all-to-all(bf16[16,8,128]{2,1,0:T(8,128)(2,1)S(1)} %shard_map.207), channel_id=1, replica_groups=mesh['rep'=32,'tp'=16] {'tp'}, dimensions={0} | all-to-all | bytes 65536 | tf_op jit(solution)/shard_map/all_to_all | solution.py:571
  82.3 0.1 shard_map.208
  82.4 15.2 %all_to_all.32.recv = bf16[16,8,128]{2,1,0:T(8,128)(2,1)S(1)} all-to-all(bf16[16,8,128]{2,1,0:T(8,128)(2,1)S(1)} %get-tuple-element.48), channel_id=1, replica_groups=mesh['rep'=32,'tp'=16] {'tp'}, dimensions={0} | all-to-all | bytes 65536 | tf_op jit(solution)/shard_map/all_to_all | solution.py:578
  97.6 0.5 shard_map.209
  98.1 15.2 %all_to_all.33.recv = bf16[16,8,128]{2,1,0:T(8,128)(2,1)S(1)} all-to-all(bf16[16,8,128]{2,1,0:T(8,128)(2,1)S(1)} %shard_map.209), channel_id=1, replica_groups=mesh['rep'=32,'tp'=16] {'tp'}, dimensions={0} | all-to-all | bytes 65536 | tf_op jit(solution)/shard_map/all_to_all | solution.py:583
  113.3 0.6 shard_map.210
  113.9 3.5 %all-to-all-start.5 = ((bf16[16,8,128]{2,1,0:T(8,128)(2,1)}), bf16[16,8,128]{2,1,0:T(8,128)(2,1)S(1)}, u32[]{:S(2)}, u32[]{:S(2)}) async-start(bf16[16,8,128]{2,1,0:T(8,128)(2,1)} %shard_map.210), calls=%async_computation.5 | async-start | bytes 65536 | tf_op jit(solution)/shard_map/all_to_all | solution.py:586
  117.4 0.0 all-gather.3.cloned.1.call-done
  117.4 2.7 %shard_map.211 = (bf16[16,128,256]{2,1,0:T(8,128)(2,1)}, f32[16,64,128]{2,1,0:T(8,128)}, f32[32,8,128]{2,1,0:T(8,128)S(1)}) custom-call(s32[2,16]{1,0:T(2,128)} %bitcast.28, s32[1,2]{1,0:T(1,128)} %slots_hbm.3, bf16[16,128,256]{2,1,0:T(8,128)(2,1)} %get-tuple-element.53.pool, ...), custom_call_target="tpu_custom_call", output_to_operand_aliasing={{0}: (2, {}), {1}: (3, {})} | custom-call | tf_op jit(solution)/shard_map/pallas_call | solution.py:588
  120.2 9.8 %all-to-all-done.5.rows_all = bf16[16,8,128]{2,1,0:T(8,128)(2,1)S(1)} async-done(((bf16[16,8,128]{2,1,0:T(8,128)(2,1)}), bf16[16,8,128]{2,1,0:T(8,128)(2,1)S(1)}, u32[]{:S(2)}, u32[]{:S(2)}) %all-to-all-start.5) | async-done | bytes 32800 | tf_op jit(solution)/shard_map/all_to_all | solution.py:586
  130.0 0.7 shard_map.212
Async XLA Ops:
  9.4 27.9 %all-to-all-start = ((bf16[16,16,128]{2,1,0:T(8,128)(2,1)}), bf16[16,16,128]{2,1,0:T(8,128)(2,1)S(1)}, u32[]{:S(2)}, u32[]{:S(2)}) async-start(bf16[16,16,128]{2,1,0:T(8,128)(2,1)} %get-tuple-element.31), calls=%async_computation | async-start | bytes 131072 | tf_op jit(solution)/shard_map/all_to_all | solution.py:496
  24.6 92.8 %all-gather.3.cloned.1.call-start = ((), (), s32[]{:S(2)}) async-start(), calls=%async_computation.6 | async-start | bytes 5541888 | tf_op jit(solution)/shard_map/all_gather | solution.py:550
  26.6 0.7 copy-start
  38.5 14.3 %collective-permute-start = (f32[16,128]{1,0:T(8,128)S(1)}, f32[16,128]{1,0:T(8,128)S(1)}, u32[]{:S(2)}, u32[]{:S(2)}) collective-permute-start(f32[16,128]{1,0:T(8,128)S(1)} %get-tuple-element.40), channel_id=1, source_target_pairs={{0,8},{1,9},{2,10},{3,11},{4,12},{5,13},{6,14},{7,15},{8,0},{9,1},... | collective-permute-start | bytes 24584 | tf_op jit(solution)/shard_map/ppermute | solution.py:551
  113.9 16.1 %all-to-all-start.5 = ((bf16[16,8,128]{2,1,0:T(8,128)(2,1)}), bf16[16,8,128]{2,1,0:T(8,128)(2,1)S(1)}, u32[]{:S(2)}, u32[]{:S(2)}) async-start(bf16[16,8,128]{2,1,0:T(8,128)(2,1)} %shard_map.210), calls=%async_computation.5 | async-start | bytes 65536 | tf_op jit(solution)/shard_map/all_to_all | solution.py:586
Sparse Core Ops, SparseCore 0:
  38.6 54.8 all-gather.2
